TPU v7x, 256 devices: a whole 4x4x8 slice. The times are simulated.
256 devices in a mesh: rows: 64 (over y, z, core), rhs: 4 (over x).
Axes of the slice: x: 4, y: 4, z: 8, core: 2. Of those that a mesh axis runs over, the one named last changes fastest.
Arguments:
- factor_left: bfloat16 [8192, 128, 128], P(('rows', 'rhs')), may hold values from -0.5 to 0.5
- factor_right: bfloat16 [8192, 128, 128], P(('rows', 'rhs')), may hold values from -0.5 to 0.5
- state_diag: float32 [8192, 128], P(('rows', 'rhs')), may hold values from 0.02 to 0.2
- owner: int32 [8192, 1], P(('rows', 'rhs')), may hold values from 0 to 63; in each aligned block of 32 rows (0 to 31, 32 to 63, ...) at most 2 rows name the same one
- col_local: int32 [8192], P(('rows', 'rhs')), may hold values from 0 to 15
- row_shift: int32 [8192], P(('rows', 'rhs')), may hold values from 0 to 2
- row_local: int32 [8192], P(('rows', 'rhs')), may hold values from 0 to 15
- rhs_in: float32 [1024, 256, 128], P('rows', 'rhs'), may hold values from -6 to 6
- low_bound: float32 [1], replicated, may hold values from 0.55 to 0.7
- high_bound: float32 [1], replicated, may hold values from 1.3 to 1.5
Outputs:
- adjoint: float32 [1024, 256, 128], P('rows', 'rhs')
- residual: float32 [1024, 256, 128], P('rows', 'rhs')
Inputs may be any that keep to these rules, and one draw needn't show every extreme that they name: Among the 32 blocks of one device no owner is named more than 2 times, and every draw has a device that names some owner 2 times.
All inputs are finite; a program needn't handle non-finite values.
Results may differ from a plain program's by a relative error of at most 0.0082.
Values may be sent and summed in bfloat16 or wider, within the bound.
No kernel may reach another device: no remote copies, remote signals or barrier semaphores. Data moves between devices by JAX's collectives and lax.ppermute only.
A program may use at most 128 MiB of HBM per device.

v0:
```python
import functools

import jax
import jax.numpy as jnp
from jax import lax
from jax.experimental import pallas as pl
from jax.experimental.pallas import tpu as pltpu
from jax.sharding import PartitionSpec as P

ITERS = 4
CHUNK = 32


def form_kernel(owner, place, left, right, diag, out0, out1, held, sems):
    slots = left.shape[0]
    columns = diag[...].T

    def target(k, out):
        return pltpu.make_async_copy(held.at[k], out.at[owner[k]], sems.at[k])

    for k in range(slots):
        scaled = (columns[:, k : k + 1] * right[k].astype(jnp.float32)).astype(jnp.bfloat16)
        held[k] = jnp.dot(left[k], scaled, preferred_element_type=jnp.float32).astype(jnp.bfloat16)

        @pl.when(place[k] == 0)
        def _():
            target(k, out0).start()

        @pl.when(place[k] != 0)
        def _():
            target(k, out1).start()

    for k in range(slots):
        target(k, out0).wait()


def form_blocks(left, right, diag, owner, place, peers):
    slots, width = diag.shape
    shape = jax.ShapeDtypeStruct((peers, width, width), jnp.bfloat16)
    return pl.pallas_call(
        form_kernel,
        out_shape=(shape, shape),
        grid_spec=pltpu.PrefetchScalarGridSpec(
            num_scalar_prefetch=2,
            in_specs=[pl.BlockSpec(memory_space=pltpu.VMEM)] * 3,
            out_specs=[pl.BlockSpec(memory_space=pltpu.HBM)] * 2,
            scratch_shapes=[
                pltpu.VMEM((slots, width, width), jnp.bfloat16),
                pltpu.SemaphoreType.DMA((slots,)),
            ],
        ),
        name="form_blocks",
    )(owner, place, left, right, diag)


def pack_kernel(order, count, got, packed, sems):
    def begin(j, carry):
        pltpu.make_async_copy(got.at[order[j]], packed.at[j], sems.at[j]).start()
        return carry

    def finish(j, carry):
        pltpu.make_async_copy(got.at[0], packed.at[0], sems.at[j]).wait()
        return carry

    lax.fori_loop(0, count[0], begin, 0)
    lax.fori_loop(0, count[0], finish, 0)


def pack_blocks(got, order, count):
    peers, width, _ = got.shape
    return pl.pallas_call(
        pack_kernel,
        out_shape=jax.ShapeDtypeStruct((peers, width, width), jnp.bfloat16),
        grid_spec=pltpu.PrefetchScalarGridSpec(
            num_scalar_prefetch=2,
            in_specs=[pl.BlockSpec(memory_space=pltpu.VMEM)],
            out_specs=pl.BlockSpec(memory_space=pltpu.HBM),
            scratch_shapes=[pltpu.SemaphoreType.DMA((peers,))],
        ),
        name="pack_blocks",
    )(order, count, got)


def read_bits(rows):
    return (3 * rows - 1).bit_length()


def sweep_kernel(num_parts, half, chunk, has_acc, last, final, *refs):
    counts, codes, coef = refs[:3]
    refs = refs[3:]
    parts, refs = refs[:num_parts], refs[num_parts:]
    fields, refs = refs[:3], refs[3:]
    num_state = 3 * last + has_acc
    state, refs = refs[:num_state], refs[num_state:]
    num_outs = (2 if final else 4) if last else 1
    outs, refs = refs[:num_outs], refs[num_outs:]
    ext, acc, held, kept, rounded, sems, field_sems, state_sems, out_sems = refs
    rows = fields[1].shape[0]
    steps = half // chunk
    halves = [(part, i) for part in parts for i in range(0, part.shape[0], half)]
    bits = read_bits(rows)
    field_copies = [
        pltpu.make_async_copy(field, ext.at[pl.ds(i * rows, rows)], field_sems.at[i])
        for i, field in enumerate(fields)
    ]
    for copy in field_copies:
        copy.start()
    for a, (part, first) in enumerate(halves):
        for c in range(steps):

            @pl.when(counts[a] > c * chunk)
            def _():
                pltpu.make_async_copy(
                    part.at[pl.ds(first + c * chunk, chunk)],
                    held.at[pl.ds(a * half + c * chunk, chunk)],
                    sems.at[a * steps + c],
                ).start()

    used = acc.at[pl.ds(1, rows)]
    state_copies = [
        pltpu.make_async_copy(array, kept.at[i], state_sems.at[i])
        for i, array in enumerate(state[: 3 * last])
    ]
    if has_acc:
        acc_copy = pltpu.make_async_copy(state[-1], used, state_sems.at[3])
        acc_copy.start()
    else:
        used[...] = jnp.zeros(used.shape, jnp.float32)
    acc[0] = jnp.zeros(acc.shape[1:], jnp.float32)
    for copy in state_copies:
        copy.start()
    for copy in field_copies:
        copy.wait()
    if has_acc:
        acc_copy.wait()

    def part_body(a, carry):
        def chunk_body(c, inner):
            base = a * half + c * chunk
            pltpu.make_async_copy(
                parts[0].at[pl.ds(0, chunk)], held.at[pl.ds(base, chunk)], sems.at[a * steps + c]
            ).wait()
            for j in range(chunk):
                code = codes[base + j]
                picked = ext[code & (2**bits - 1)]
                acc[code >> bits] += jnp.dot(
                    picked, held[base + j], preferred_element_type=jnp.float32
                )
            return inner

        return lax.fori_loop(0, lax.div(counts[a] + chunk - 1, chunk), chunk_body, carry)

    lax.fori_loop(0, len(halves), part_body, 0)

    if not last:
        results = [used]
    else:
        for copy in state_copies:
            copy.wait()
        adjoint, residual, direction = (kept.at[i] for i in range(3))
        step = direction[...]
        left = residual[...] - (step - used[...])
        residual[...] = left
        results = [adjoint, residual]
        if not final:
            step = coef[0] * step + coef[1] * left
            rounded[...] = step.astype(jnp.bfloat16)
            direction[...] = step
            adjoint[...] = adjoint[...] + step
            results = [rounded, adjoint, residual, direction]
    out_copies = [
        pltpu.make_async_copy(result, out, out_sems.at[i])
        for i, (result, out) in enumerate(zip(results, outs))
    ]
    for copy in out_copies:
        copy.start()
    for copy in out_copies:
        copy.wait()


def sweep(parts, counts, codes, coef, fields, acc_in=None, state=None, final=False):
    half, width = parts[-1].shape[:2]
    chunk = min(CHUNK, half)
    held = sum(part.shape[0] for part in parts)
    rows, columns, _ = fields[1].shape
    last = state is not None
    wide = jax.ShapeDtypeStruct((rows, columns, width), jnp.float32)
    if not last:
        outs = (wide,)
    elif final:
        outs = (wide, wide)
    else:
        outs = (jax.ShapeDtypeStruct(wide.shape, jnp.bfloat16), wide, wide, wide)
    extra = list(fields) + list(state or ()) + ([acc_in] if acc_in is not None else [])
    return pl.pallas_call(
        functools.partial(sweep_kernel, len(parts), half, chunk, acc_in is not None, last, final),
        out_shape=outs,
        in_specs=[pl.BlockSpec(memory_space=pltpu.SMEM)] * 3
        + [pl.BlockSpec(memory_space=pltpu.HBM)] * (len(parts) + len(extra)),
        out_specs=[pl.BlockSpec(memory_space=pltpu.HBM)] * len(outs),
        scratch_shapes=[
            pltpu.VMEM((3 * rows, columns, width), jnp.bfloat16),
            pltpu.VMEM((rows + 1, columns, width), jnp.float32),
            pltpu.VMEM((held, width, width), jnp.bfloat16),
            pltpu.VMEM((3, rows, columns, width), jnp.float32),
            pltpu.VMEM((rows, columns, width), jnp.bfloat16),
            pltpu.SemaphoreType.DMA((held // chunk,)),
            pltpu.SemaphoreType.DMA((3,)),
            pltpu.SemaphoreType.DMA((4,)),
            pltpu.SemaphoreType.DMA((4,)),
        ],
        compiler_params=pltpu.CompilerParams(vmem_limit_bytes=60 * 2**20),
        name="sweep",
    )(counts, codes, coef, *parts, *extra)


def ring(count, shift):
    return [(i, (i + shift) % count) for i in range(count)]


def near(packed):
    count = lax.axis_size("rhs")
    return (
        lax.ppermute(packed, "rhs", ring(count, 1)),
        lax.ppermute(packed, "rhs", ring(count, -1)),
    )


def far(above, below):
    count = lax.axis_size("rhs")
    half = above.shape[0] // 2
    return (
        lax.ppermute(above[:half], "rhs", ring(count, 1)),
        lax.ppermute(below[half:], "rhs", ring(count, -1)),
    )


def neighbours(rounded):
    count = lax.axis_size("rows")
    return (
        lax.ppermute(rounded, "rows", ring(count, 1)),
        rounded,
        lax.ppermute(rounded, "rows", ring(count, -1)),
    )


def local_program(
    factor_left,
    factor_right,
    state_diag,
    owner,
    col_local,
    row_shift,
    row_local,
    rhs_in,
    low_bound,
    high_bound,
):
    peers = lax.axis_size("rows")
    across = lax.axis_size("rhs")
    slots = owner.shape[0]
    local_rows = rhs_in.shape[0]
    bits = read_bits(local_rows)
    dest = owner[:, 0]
    order = jnp.arange(slots)
    earlier = (dest[:, None] == dest[None, :]) & (order[None, :] < order[:, None])
    place = jnp.sum(earlier.astype(jnp.int32), axis=1)
    code = ((col_local + 1) << bits) + row_shift * local_rows + row_local
    spot = dest * 2 + place
    send_codes = jnp.sum(
        jnp.where(jnp.arange(2 * peers)[:, None] == spot[None, :], code[None, :], 0), axis=1
    )
    got_codes = lax.all_to_all(
        send_codes.reshape(peers, 2), "rows", split_axis=0, concat_axis=0, tiled=True
    ).T
    number = jnp.arange(peers)
    key = jnp.where(got_codes > 0, got_codes, jnp.int32(1 << 20))
    ahead = (key[:, None, :] < key[:, :, None]) | (
        (key[:, None, :] == key[:, :, None]) & (number[None, None, :] < number[None, :, None])
    )
    rank = jnp.sum(ahead.astype(jnp.int32), axis=2)
    chosen = rank[:, None, :] == number[None, :, None]
    source = jnp.sum(jnp.where(chosen, number[None, None, :], 0), axis=2)
    sorted_codes = jnp.sum(jnp.where(chosen, got_codes[:, None, :], 0), axis=2)
    count = jnp.sum((got_codes > 0).astype(jnp.int32), axis=1)

    up = lax.ppermute(sorted_codes, "rhs", ring(across, 1))
    down = lax.ppermute(sorted_codes, "rhs", ring(across, -1))
    far_codes = lax.ppermute(sorted_codes, "rhs", ring(across, 2))
    all_codes = jnp.stack([sorted_codes, up, down, far_codes], axis=1)
    all_codes = all_codes.reshape(2, 4, 2, peers // 2)
    all_counts = jnp.sum((all_codes > 0).astype(jnp.int32), axis=3).reshape(2, 8)
    all_codes = all_codes.reshape(2, 4 * peers)
    low = low_bound[0]
    high = high_bound[0]
    theta = (high + low) / 2.0
    delta = (high - low) / 2.0
    sigma = theta / delta
    rho = 1.0 / sigma
    coefs = []
    for number in range(ITERS):
        rho_next = 1.0 / (2.0 * sigma - rho)
        coefs.append(jnp.stack([rho_next * rho, 2.0 * rho_next / delta]))
        rho = rho_next
    tables = (
        source[1],
        count[1:],
        all_counts[0],
        all_counts[1],
        all_counts.reshape(16),
        all_codes[0],
        all_codes[1],
        all_codes.reshape(8 * peers),
        *coefs,
    )

    sent0, sent1 = form_blocks(factor_left, factor_right, state_diag, dest, place, peers)
    got0 = lax.all_to_all(sent0, "rows", split_axis=0, concat_axis=0, tiled=True)
    packed0 = pack_blocks(got0, source[0], count[:1])
    near0 = near(packed0)
    far0 = far(*near0)
    sent1, _, *tables = lax.optimization_barrier((sent1, packed0, *tables))
    order1, number1, counts0, counts1, counts, codes0, codes1, codes, *coefs = tables
    got1 = lax.all_to_all(sent1, "rows", split_axis=0, concat_axis=0, tiled=True)
    packed1 = pack_blocks(got1, order1, number1)

    residual = rhs_in
    direction = residual / theta
    adjoint = direction
    fields = neighbours(direction.astype(jnp.bfloat16))

    def first_product(parts):
        (acc,) = sweep(parts, counts0, codes0, coefs[0], fields)
        return acc

    def with_second(parts, packed):
        near1 = near(packed)
        acc = first_product(parts)
        return acc, [packed, *near1, *far(*near1)]

    def without_second(parts, packed):
        half = packed.shape[0] // 2
        return first_product(parts), [packed, packed, packed, packed[:half], packed[half:]]

    parts0 = [packed0, *near0, *far0]
    acc, parts1 = lax.cond(jnp.sum(counts1) > 0, with_second, without_second, parts0, packed1)
    for number in range(ITERS):
        state = (adjoint, residual, direction)
        final = number + 1 == ITERS
        if number == 0:
            out = sweep(parts1, counts1, codes1, coefs[0], fields, acc, state)
        else:
            out = sweep(
                parts0 + parts1, counts, codes, coefs[number], fields, None, state, final
            )
        if final:
            return out
        rounded, adjoint, residual, direction = out
        fields = neighbours(rounded)


def solution(mesh):
    placed = (
        P(("rows", "rhs"), None, None),
        P(("rows", "rhs"), None, None),
        P(("rows", "rhs"), None),
        P(("rows", "rhs"), None),
        P(("rows", "rhs")),
        P(("rows", "rhs")),
        P(("rows", "rhs")),
        P("rows", "rhs", None),
        P(),
        P(),
    )
    return jax.shard_map(
        local_program,
        mesh=mesh,
        in_specs=placed,
        out_specs=(P("rows", "rhs", None), P("rows", "rhs", None)),
        check_vma=False,
    )
```

profile of v0, /device:TPU:32, one launch (start us, length us, event | category | flops | bytes accessed | tf_op | source)
XLA Modules:
  0.0 312.8 jit_solution(16276516234774136705)
XLA Ops:
  3.8 11.8 %all-to-all-start = ((s32[64,1,2]{2,1,0:T(1,128)}), s32[64,1,2]{2,1,0:T(1,128)S(1)}, u32[]{:S(2)}, u32[]{:S(2)}) async-start(s32[64,1,2]{2,1,0:T(1,128)} %bitcast.1), calls=%async_computation | async-start | bytes 65536 | tf_op jit(solution)/shard_map/all_to_all | solution.py:273
  15.5 4.1 %form_blocks.1 = (bf16[64,128,128]{2,1,0:T(8,128)(2,1)}, bf16[64,128,128]{2,1,0:T(8,128)(2,1)}) custom-call(s32[32]{0:T(128)} %bitcast.32, s32[32]{0:T(128)} %copy-done.12, bf16[32,128,128]{2,1,0:T(8,128)(2,1)} %left.1, bf16[32,128,128]{2,1,0:T(8,128)(2,1)} %right.1, f32[32,128]{1,0:T(8,128)} %diag.1), custom_call_target="tpu_custom_call" | custom-call | tf_op jit(solution)/shard_map/form_blocks/pallas_call | solution.py:40
  19.7 4.3 %all-to-all-done = s32[64,1,2]{2,1,0:T(1,128)S(1)} async-done(((s32[64,1,2]{2,1,0:T(1,128)}), s32[64,1,2]{2,1,0:T(1,128)S(1)}, u32[]{:S(2)}, u32[]{:S(2)}) %all-to-all-start) | async-done | bytes 544 | tf_op jit(solution)/shard_map/all_to_all | solution.py:273
  24.0 6.0 %all-to-all-start.1 = ((bf16[64,128,128]{2,1,0:T(8,128)(2,1)}), bf16[64,128,128]{2,1,0:T(8,128)(2,1)S(1)}, u32[]{:S(2)}, u32[]{:S(2)}) async-start(bf16[64,128,128]{2,1,0:T(8,128)(2,1)} %get-tuple-element.107), calls=%async_computation.1 | async-start | bytes 4194304 | tf_op jit(solution)/shard_map/all_to_all | solution.py:318
  33.4 3.1 %collective-permute-start.6 = (s32[2,64]{1,0:T(2,128)S(1)}, s32[2,64]{1,0:T(2,128)S(1)}, u32[]{:S(2)}, u32[]{:S(2)}) collective-permute-start(s32[2,64]{1,0:T(2,128)S(1)} %get-tuple-element.142), channel_id=1, source_target_pairs={{0,2},{1,3},{2,0},{3,1},{4,6},{5,7},{6,4},{7,5},{8,10},{9,11},{10,... | collective-permute-start | bytes 1544 | tf_op jit(solution)/shard_map/ppermute | solution.py:289
  40.2 2.2 collective-permute-done.4
  45.1 34.6 %all-to-all-done.1.got = bf16[64,128,128]{2,1,0:T(8,128)(2,1)S(1)} async-done(((bf16[64,128,128]{2,1,0:T(8,128)(2,1)}), bf16[64,128,128]{2,1,0:T(8,128)(2,1)S(1)}, u32[]{:S(2)}, u32[]{:S(2)}) %all-to-all-start.1) | async-done | bytes 2097184 | tf_op jit(solution)/shard_map/all_to_all | solution.py:318
  81.0 7.1 %pack_blocks.2.refs_3_ = bf16[64,128,128]{2,1,0:T(8,128)(2,1)S(1)} custom-call(s32[64]{0:T(128)} %get-tuple-element.149.order, s32[1]{0:T(128)} %get-tuple-element.153.count, bf16[64,128,128]{2,1,0:T(8,128)(2,1)} %copy-done.3), custom_call_target="tpu_custom_call" | custom-call | tf_op jit(solution)/shard_map/pack_blocks/pallas_call | solution.py:71
  88.2 6.4 %all-to-all-start.2 = ((bf16[64,128,128]{2,1,0:T(8,128)(2,1)}), bf16[64,128,128]{2,1,0:T(8,128)(2,1)}, u32[]{:S(2)}, u32[]{:S(2)}) async-start(bf16[64,128,128]{2,1,0:T(8,128)(2,1)} %get-tuple-element.113), calls=%async_computation.2 | async-start | bytes 4194304 | tf_op jit(solution)/shard_map/all_to_all | solution.py:324
  94.6 2.8 collective-permute-start.8
  97.4 45.2 %collective-permute-done.8.refs_5_ = bf16[64,128,128]{2,1,0:T(8,128)(2,1)S(1)} collective-permute-done((bf16[64,128,128]{2,1,0:T(8,128)(2,1)S(1)}, bf16[64,128,128]{2,1,0:T(8,128)(2,1)S(1)}, u32[]{:S(2)}, u32[]{:S(2)}) %collective-permute-start.8) | collective-permute-done | bytes 2097184 | tf_op jit(solution)/shard_map/ppermute | solution.py:225
  143.8 3.7 %collective-permute-start.10 = (bf16[32,128,128]{2,1,0:T(8,128)(2,1)}, bf16[32,128,128]{2,1,0:T(8,128)(2,1)S(1)}, u32[]{:S(2)}, u32[]{:S(2)}) collective-permute-start(bf16[32,128,128]{2,1,0:T(8,128)(2,1)} %slice.63), channel_id=1, source_target_pairs={{0,3},{1,0},{2,1},{3,2},{4,7},{5,4},{6,5},{7,6},{8,11},{9,8},{10,9... | collective-permute-start | bytes 3145736 | tf_op jit(solution)/shard_map/ppermute | solution.py:234
  151.9 7.0 %pack_blocks.3.refs_3_.refs_8_ = bf16[64,128,128]{2,1,0:T(8,128)(2,1)S(1)} custom-call(s32[64]{0:T(128)} %get-tuple-element.111.order, s32[1]{0:T(128)} %get-tuple-element.112.count, bf16[64,128,128]{2,1,0:T(8,128)(2,1)} %all-to-all-done.2.got), custom_call_target="tpu_custom_call" | custom-call | tf_op jit(solution)/shard_map/pack_blocks/pallas_call | solution.py:71
  158.9 10.9 %collective-permute-done.10.refs_7_ = bf16[32,128,128]{2,1,0:T(8,128)(2,1)S(1)} collective-permute-done((bf16[32,128,128]{2,1,0:T(8,128)(2,1)}, bf16[32,128,128]{2,1,0:T(8,128)(2,1)S(1)}, u32[]{:S(2)}, u32[]{:S(2)}) %collective-permute-start.10) | collective-permute-done | bytes 1048608 | tf_op jit(solution)/shard_map/ppermute | solution.py:234
  169.7 4.6 %collective-permute-done.9.refs_6_ = bf16[32,128,128]{2,1,0:T(8,128)(2,1)} collective-permute-done((bf16[32,128,128]{2,1,0:T(8,128)(2,1)}, bf16[32,128,128]{2,1,0:T(8,128)(2,1)}, u32[]{:S(2)}, u32[]{:S(2)}) %collective-permute-start.9) | collective-permute-done | bytes 1048608 | tf_op jit(solution)/shard_map/ppermute | solution.py:233
  174.3 76.0 %conditional.1 = (f32[16,64,128]{2,1,0:T(8,128)S(1)}, bf16[64,128,128]{2,1,0:T(8,128)(2,1)}, bf16[64,128,128]{2,1,0:T(8,128)(2,1)}, bf16[32,128,128]{2,1,0:T(8,128)(2,1)}, bf16[32,128,128]{2,1,0:T(8,128)(2,1)}) conditional(s32[]{:T(128)} %convert_element_type.22, (s32[8]{0:T(128)S(1)}, s32[256]{0:T(256)S(1)}, f32[2]{0:T(128)S(1)}, ...), branch_computations={%region_8.9_spmd, %region_9.10_spmd} | conditional | bytes 29360328 | solution.py:346
  174.3 2.0 collective-permute-start
  176.4 43.8 %collective-permute-done.1 = bf16[64,128,128]{2,1,0:T(8,128)(2,1)} collective-permute-done((bf16[64,128,128]{2,1,0:T(8,128)(2,1)S(1)}, bf16[64,128,128]{2,1,0:T(8,128)(2,1)}, u32[]{:S(2)}, u32[]{:S(2)}) %collective-permute-start.1) | collective-permute-done | bytes 2097184 | tf_op jit(solution)/shard_map/cond/branch_1_fun/ppermute | solution.py:225
  220.2 2.3 slice.57
  224.0 2.3 slice.56
  226.9 6.8 %sweep.7 = f32[16,64,128]{2,1,0:T(8,128)S(1)} custom-call(s32[8]{0:T(128)S(1)} %get-tuple-element.60.refs_0_, s32[256]{0:T(256)S(1)} %get-tuple-element.61.refs_1_, f32[2]{0:T(128)S(1)} %get-tuple-element.62.refs_2_, bf16[64,128,128]{2,1,0:T(8,128)(2,1)} %get-tuple-element.63.refs_3_, bf16[64,128,128]{2,1,0:T(8,128)(2,1)} %get-tuple-element.64.refs_4_, ...), custom_call_target="tpu_custom_call" | custom-call | tf_op jit(solution)/shard_map/cond/branch_1_fun/sweep/pallas_call | solution.py:195
  233.8 11.5 %collective-permute-done.3 = bf16[32,128,128]{2,1,0:T(8,128)(2,1)} collective-permute-done((bf16[32,128,128]{2,1,0:T(8,128)(2,1)}, bf16[32,128,128]{2,1,0:T(8,128)(2,1)}, u32[]{:S(2)}, u32[]{:S(2)}) %collective-permute-start.3) | collective-permute-done | bytes 1048608 | tf_op jit(solution)/shard_map/cond/branch_1_fun/ppermute | solution.py:234
  245.3 5.0 %collective-permute-done.2 = bf16[32,128,128]{2,1,0:T(8,128)(2,1)} collective-permute-done((bf16[32,128,128]{2,1,0:T(8,128)(2,1)}, bf16[32,128,128]{2,1,0:T(8,128)(2,1)}, u32[]{:S(2)}, u32[]{:S(2)}) %collective-permute-start.2) | collective-permute-done | bytes 1048608 | tf_op jit(solution)/shard_map/cond/branch_1_fun/ppermute | solution.py:233
  250.3 6.7 %sweep.8 = (bf16[16,64,128]{2,1,0:T(8,128)(2,1)}, f32[16,64,128]{2,1,0:T(8,128)}, f32[16,64,128]{2,1,0:T(8,128)}, f32[16,64,128]{2,1,0:T(8,128)}) custom-call(s32[8]{0:T(128)} %copy-done.11, s32[256]{0:T(256)} %squeeze.29.refs_1_, f32[2]{0:T(128)S(1)} %get-tuple-element.117.refs_2_, bf16[64,128,128]{2,1,0:T(8,128)(2,1)S(1)} %pack_blocks.3.refs_3_.refs_8_, ...), custom_call_target="tpu_custom_call" | custom-call | tf_op jit(solution)/shard_map/sweep/pallas_call | solution.py:195
  257.7 3.7 %collective-permute-done.14.refs_15_ = bf16[16,64,128]{2,1,0:T(8,128)(2,1)S(1)} collective-permute-done((bf16[16,64,128]{2,1,0:T(8,128)(2,1)}, bf16[16,64,128]{2,1,0:T(8,128)(2,1)S(1)}, u32[]{:S(2)}, u32[]{:S(2)}) %collective-permute-start.14) | collective-permute-done | bytes 262176 | tf_op jit(solution)/shard_map/ppermute | solution.py:243
  261.4 1.9 collective-permute-done.13.refs_13_
  263.9 11.6 %sweep.9 = (bf16[16,64,128]{2,1,0:T(8,128)(2,1)}, f32[16,64,128]{2,1,0:T(8,128)}, f32[16,64,128]{2,1,0:T(8,128)}, f32[16,64,128]{2,1,0:T(8,128)}) custom-call(s32[16]{0:T(128)} %reshape_reshape.4.refs_0_, s32[512]{0:T(512)} %reshape_reshape_reshape.3.refs_1_, f32[2]{0:T(128)} %get-tuple-element.123.refs_2_, bf16[64,128,128]{2,1,0:T(8,128)(2,1)} %copy-done, ...), custom_call_target="tpu_custom_call" | custom-call | tf_op jit(solution)/shard_map/sweep/pallas_call | solution.py:195
  276.2 3.7 %collective-permute-done.16.refs_15_ = bf16[16,64,128]{2,1,0:T(8,128)(2,1)S(1)} collective-permute-done((bf16[16,64,128]{2,1,0:T(8,128)(2,1)}, bf16[16,64,128]{2,1,0:T(8,128)(2,1)S(1)}, u32[]{:S(2)}, u32[]{:S(2)}) %collective-permute-start.16) | collective-permute-done | bytes 262176 | tf_op jit(solution)/shard_map/ppermute | solution.py:243
  279.9 1.9 collective-permute-done.15.refs_13_
  282.5 11.7 %sweep.10 = (bf16[16,64,128]{2,1,0:T(8,128)(2,1)}, f32[16,64,128]{2,1,0:T(8,128)}, f32[16,64,128]{2,1,0:T(8,128)}, f32[16,64,128]{2,1,0:T(8,128)}) custom-call(s32[16]{0:T(128)} %reshape_reshape.4.refs_0_, s32[512]{0:T(512)} %reshape_reshape_reshape.3.refs_1_, f32[2]{0:T(128)} %get-tuple-element.122.refs_2_, bf16[64,128,128]{2,1,0:T(8,128)(2,1)} %copy-done, ...), custom_call_target="tpu_custom_call" | custom-call | tf_op jit(solution)/shard_map/sweep/pallas_call | solution.py:195
  294.7 3.7 %collective-permute-done.18.refs_15_ = bf16[16,64,128]{2,1,0:T(8,128)(2,1)S(1)} collective-permute-done((bf16[16,64,128]{2,1,0:T(8,128)(2,1)}, bf16[16,64,128]{2,1,0:T(8,128)(2,1)S(1)}, u32[]{:S(2)}, u32[]{:S(2)}) %collective-permute-start.18) | collective-permute-done | bytes 262176 | tf_op jit(solution)/shard_map/ppermute | solution.py:243
  301.0 11.6 %sweep.11 = (f32[16,64,128]{2,1,0:T(8,128)}, f32[16,64,128]{2,1,0:T(8,128)}) custom-call(s32[16]{0:T(128)} %reshape_reshape.4.refs_0_, s32[512]{0:T(512)} %reshape_reshape_reshape.3.refs_1_, f32[2]{0:T(128)} %get-tuple-element.110.refs_2_, bf16[64,128,128]{2,1,0:T(8,128)(2,1)} %copy-done, bf16[64,128,128]{2,1,0:T(8,128)(2,1)} %copy-done.2, ...), custom_call_target="tpu_custom_call" | custom-call | tf_op jit(solution)/shard_map/sweep/pallas_call | solution.py:195
  (83 shorter events, 25.1 us)
Async XLA Ops:
  1.5 14.0 %copy-start.12 = (s32[32]{0:T(128)}, s32[32]{0:T(128)S(1)}, u32[]{:S(2)}) copy-start(s32[32]{0:T(128)S(1)} %convert_reduce_fusion.1.place) | copy-start | bytes 388
  3.8 20.3 %all-to-all-start = ((s32[64,1,2]{2,1,0:T(1,128)}), s32[64,1,2]{2,1,0:T(1,128)S(1)}, u32[]{:S(2)}, u32[]{:S(2)}) async-start(s32[64,1,2]{2,1,0:T(1,128)} %bitcast.1), calls=%async_computation | async-start | bytes 65536 | tf_op jit(solution)/shard_map/all_to_all | solution.py:273
  24.0 55.7 %all-to-all-start.1 = ((bf16[64,128,128]{2,1,0:T(8,128)(2,1)}), bf16[64,128,128]{2,1,0:T(8,128)(2,1)S(1)}, u32[]{:S(2)}, u32[]{:S(2)}) async-start(bf16[64,128,128]{2,1,0:T(8,128)(2,1)} %get-tuple-element.107), calls=%async_computation.1 | async-start | bytes 4194304 | tf_op jit(solution)/shard_map/all_to_all | solution.py:318
  33.4 6.4 %collective-permute-start.6 = (s32[2,64]{1,0:T(2,128)S(1)}, s32[2,64]{1,0:T(2,128)S(1)}, u32[]{:S(2)}, u32[]{:S(2)}) collective-permute-start(s32[2,64]{1,0:T(2,128)S(1)} %get-tuple-element.142), channel_id=1, source_target_pairs={{0,2},{1,3},{2,0},{3,1},{4,6},{5,7},{6,4},{7,5},{8,10},{9,11},{10,... | collective-permute-start | bytes 1544 | tf_op jit(solution)/shard_map/ppermute | solution.py:289
  36.6 3.6 %collective-permute-start.5 = (s32[2,64]{1,0:T(2,128)S(1)}, s32[2,64]{1,0:T(2,128)S(1)}, u32[]{:S(2)}, u32[]{:S(2)}) collective-permute-start(s32[2,64]{1,0:T(2,128)S(1)} %get-tuple-element.142), channel_id=1, source_target_pairs={{0,3},{1,0},{2,1},{3,2},{4,7},{5,4},{6,5},{7,6},{8,11},{9,8},{10,9... | collective-permute-start | bytes 1544 | tf_op jit(solution)/shard_map/ppermute | solution.py:288
  37.7 4.8 %collective-permute-start.4 = (s32[2,64]{1,0:T(2,128)S(1)}, s32[2,64]{1,0:T(2,128)S(1)}, u32[]{:S(2)}, u32[]{:S(2)}) collective-permute-start(s32[2,64]{1,0:T(2,128)S(1)} %get-tuple-element.142), channel_id=1, source_target_pairs={{0,1},{1,2},{2,3},{3,0},{4,5},{5,6},{6,7},{7,4},{8,9},{9,10},{10,1... | collective-permute-start | bytes 1544 | tf_op jit(solution)/shard_map/ppermute | solution.py:287
  43.6 107.0 %copy-start.11 = (s32[8]{0:T(128)}, s32[8]{0:T(128)S(1)}, u32[]{:S(2)}) copy-start(s32[8]{0:T(128)S(1)} %squeeze.27.refs_0_) | copy-start | bytes 100
  79.7 1.3 copy-start.3
  88.1 9.3 %copy-start = (bf16[64,128,128]{2,1,0:T(8,128)(2,1)}, bf16[64,128,128]{2,1,0:T(8,128)(2,1)S(1)}, u32[]{:S(2)}) copy-start(bf16[64,128,128]{2,1,0:T(8,128)(2,1)S(1)} %pack_blocks.2.refs_3_) | copy-start | bytes 6291460
  88.2 63.7 %all-to-all-start.2 = ((bf16[64,128,128]{2,1,0:T(8,128)(2,1)}), bf16[64,128,128]{2,1,0:T(8,128)(2,1)}, u32[]{:S(2)}, u32[]{:S(2)}) async-start(bf16[64,128,128]{2,1,0:T(8,128)(2,1)} %get-tuple-element.113), calls=%async_computation.2 | async-start | bytes 4194304 | tf_op jit(solution)/shard_map/all_to_all | solution.py:324
  94.6 54.6 %copy-start.4 = (f32[16,64,128]{2,1,0:T(8,128)S(1)}, f32[16,64,128]{2,1,0:T(8,128)}, u32[]{:S(2)}) copy-start(f32[16,64,128]{2,1,0:T(8,128)} %refs_12_.1) | copy-start | bytes 1572868
  94.6 48.0 %collective-permute-start.8 = (bf16[64,128,128]{2,1,0:T(8,128)(2,1)S(1)}, bf16[64,128,128]{2,1,0:T(8,128)(2,1)S(1)}, u32[]{:S(2)}, u32[]{:S(2)}) collective-permute-start(bf16[64,128,128]{2,1,0:T(8,128)(2,1)S(1)} %pack_blocks.2.refs_3_), channel_id=1, source_target_pairs={{0,3},{1,0},{2,1},{3,2},{4,7},{5,4},{6,5},{7,6},{8,11},{9,8},{10,9... | collective-permute-start | bytes 6291464 | tf_op jit(solution)/shard_map/ppermute | solution.py:225
  97.4 50.1 %collective-permute-start.7 = (bf16[64,128,128]{2,1,0:T(8,128)(2,1)S(1)}, bf16[64,128,128]{2,1,0:T(8,128)(2,1)S(1)}, u32[]{:S(2)}, u32[]{:S(2)}) collective-permute-start(bf16[64,128,128]{2,1,0:T(8,128)(2,1)S(1)} %pack_blocks.2.refs_3_), channel_id=1, source_target_pairs={{0,1},{1,2},{2,3},{3,0},{4,5},{5,6},{6,7},{7,4},{8,9},{9,10},{10,1... | collective-permute-start | bytes 6291464 | tf_op jit(solution)/shard_map/ppermute | solution.py:224
  142.6 6.1 %copy-start.1 = (bf16[64,128,128]{2,1,0:T(8,128)(2,1)}, bf16[64,128,128]{2,1,0:T(8,128)(2,1)S(1)}, u32[]{:S(2)}) copy-start(bf16[64,128,128]{2,1,0:T(8,128)(2,1)S(1)} %collective-permute-done.8.refs_5_) | copy-start | bytes 6291460
  143.8 26.0 %collective-permute-start.10 = (bf16[32,128,128]{2,1,0:T(8,128)(2,1)}, bf16[32,128,128]{2,1,0:T(8,128)(2,1)S(1)}, u32[]{:S(2)}, u32[]{:S(2)}) collective-permute-start(bf16[32,128,128]{2,1,0:T(8,128)(2,1)} %slice.63), channel_id=1, source_target_pairs={{0,3},{1,0},{2,1},{3,2},{4,7},{5,4},{6,5},{7,6},{8,11},{9,8},{10,9... | collective-permute-start | bytes 3145736 | tf_op jit(solution)/shard_map/ppermute | solution.py:234
  147.5 1.7 copy-start.2
  148.7 25.7 %collective-permute-start.9 = (bf16[32,128,128]{2,1,0:T(8,128)(2,1)}, bf16[32,128,128]{2,1,0:T(8,128)(2,1)}, u32[]{:S(2)}, u32[]{:S(2)}) collective-permute-start(bf16[32,128,128]{2,1,0:T(8,128)(2,1)} %slice.62), channel_id=1, source_target_pairs={{0,1},{1,2},{2,3},{3,0},{4,5},{5,6},{6,7},{7,4},{8,9},{9,10},{10,1... | collective-permute-start | bytes 3145736 | tf_op jit(solution)/shard_map/ppermute | solution.py:233
  150.1 8.8 %collective-permute-start.12 = (bf16[16,64,128]{2,1,0:T(8,128)(2,1)S(1)}, bf16[16,64,128]{2,1,0:T(8,128)(2,1)}, u32[]{:S(2)}, u32[]{:S(2)}) collective-permute-start(bf16[16,64,128]{2,1,0:T(8,128)(2,1)S(1)} %get-tuple-element.144.refs_9_), channel_id=1, source_target_pairs={{0,252},{4,0},{8,4},{12,8},{16,12},{20,16},{24,20},{28,24},{32,28}... | collective-permute-start | bytes 786440 | tf_op jit(solution)/shard_map/ppermute | solution.py:243
  150.1 8.8 %collective-permute-start.11 = (bf16[16,64,128]{2,1,0:T(8,128)(2,1)S(1)}, bf16[16,64,128]{2,1,0:T(8,128)(2,1)}, u32[]{:S(2)}, u32[]{:S(2)}) collective-permute-start(bf16[16,64,128]{2,1,0:T(8,128)(2,1)S(1)} %get-tuple-element.144.refs_9_), channel_id=1, source_target_pairs={{0,4},{4,8},{8,12},{12,16},{16,20},{20,24},{24,28},{28,32},{32,36}... | collective-permute-start | bytes 786440 | tf_op jit(solution)/shard_map/ppermute | solution.py:241
  174.3 45.9 %collective-permute-start.1 = (bf16[64,128,128]{2,1,0:T(8,128)(2,1)S(1)}, bf16[64,128,128]{2,1,0:T(8,128)(2,1)}, u32[]{:S(2)}, u32[]{:S(2)}) collective-permute-start(bf16[64,128,128]{2,1,0:T(8,128)(2,1)S(1)} %get-tuple-element.71), channel_id=1, source_target_pairs={{0,3},{1,0},{2,1},{3,2},{4,7},{5,4},{6,5},{7,6},{8,11},{9,8},{10,9... | collective-permute-start | bytes 6291464 | tf_op jit(solution)/shard_map/cond/branch_1_fun/ppermute | solution.py:225
  174.3 49.7 %collective-permute-start = (bf16[64,128,128]{2,1,0:T(8,128)(2,1)S(1)}, bf16[64,128,128]{2,1,0:T(8,128)(2,1)}, u32[]{:S(2)}, u32[]{:S(2)}) collective-permute-start(bf16[64,128,128]{2,1,0:T(8,128)(2,1)S(1)} %get-tuple-element.71), channel_id=1, source_target_pairs={{0,1},{1,2},{2,3},{3,0},{4,5},{5,6},{6,7},{7,4},{8,9},{9,10},{10,1... | collective-permute-start | bytes 6291464 | tf_op jit(solution)/shard_map/cond/branch_1_fun/ppermute | solution.py:224
  222.6 22.8 %collective-permute-start.3 = (bf16[32,128,128]{2,1,0:T(8,128)(2,1)}, bf16[32,128,128]{2,1,0:T(8,128)(2,1)}, u32[]{:S(2)}, u32[]{:S(2)}) collective-permute-start(bf16[32,128,128]{2,1,0:T(8,128)(2,1)} %slice.57), channel_id=1, source_target_pairs={{0,3},{1,0},{2,1},{3,2},{4,7},{5,4},{6,5},{7,6},{8,11},{9,8},{10,9... | collective-permute-start | bytes 3145736 | tf_op jit(solution)/shard_map/cond/branch_1_fun/ppermute | solution.py:234
  226.4 24.0 %collective-permute-start.2 = (bf16[32,128,128]{2,1,0:T(8,128)(2,1)}, bf16[32,128,128]{2,1,0:T(8,128)(2,1)}, u32[]{:S(2)}, u32[]{:S(2)}) collective-permute-start(bf16[32,128,128]{2,1,0:T(8,128)(2,1)} %slice.56), channel_id=1, source_target_pairs={{0,1},{1,2},{2,3},{3,0},{4,5},{5,6},{6,7},{7,4},{8,9},{9,10},{10,1... | collective-permute-start | bytes 3145736 | tf_op jit(solution)/shard_map/cond/branch_1_fun/ppermute | solution.py:233
  257.1 4.3 %collective-permute-start.14 = (bf16[16,64,128]{2,1,0:T(8,128)(2,1)}, bf16[16,64,128]{2,1,0:T(8,128)(2,1)S(1)}, u32[]{:S(2)}, u32[]{:S(2)}) collective-permute-start(bf16[16,64,128]{2,1,0:T(8,128)(2,1)} %get-tuple-element.126.refs_14_), channel_id=1, source_target_pairs={{0,252},{4,0},{8,4},{12,8},{16,12},{20,16},{24,20},{28,24},{32,28}... | collective-permute-start | bytes 786440 | tf_op jit(solution)/shard_map/ppermute | solution.py:243
  257.2 6.1 %collective-permute-start.13 = (bf16[16,64,128]{2,1,0:T(8,128)(2,1)}, bf16[16,64,128]{2,1,0:T(8,128)(2,1)S(1)}, u32[]{:S(2)}, u32[]{:S(2)}) collective-permute-start(bf16[16,64,128]{2,1,0:T(8,128)(2,1)} %get-tuple-element.126.refs_14_), channel_id=1, source_target_pairs={{0,4},{4,8},{8,12},{12,16},{16,20},{20,24},{24,28},{28,32},{32,36}... | collective-permute-start | bytes 786440 | tf_op jit(solution)/shard_map/ppermute | solution.py:241
  261.4 1.9 copy-start.7
  275.6 4.3 %collective-permute-start.16 = (bf16[16,64,128]{2,1,0:T(8,128)(2,1)}, bf16[16,64,128]{2,1,0:T(8,128)(2,1)S(1)}, u32[]{:S(2)}, u32[]{:S(2)}) collective-permute-start(bf16[16,64,128]{2,1,0:T(8,128)(2,1)} %get-tuple-element.130.refs_14_), channel_id=1, source_target_pairs={{0,252},{4,0},{8,4},{12,8},{16,12},{20,16},{24,20},{28,24},{32,28}... | collective-permute-start | bytes 786440 | tf_op jit(solution)/shard_map/ppermute | solution.py:243
  275.7 6.1 %collective-permute-start.15 = (bf16[16,64,128]{2,1,0:T(8,128)(2,1)}, bf16[16,64,128]{2,1,0:T(8,128)(2,1)S(1)}, u32[]{:S(2)}, u32[]{:S(2)}) collective-permute-start(bf16[16,64,128]{2,1,0:T(8,128)(2,1)} %get-tuple-element.130.refs_14_), channel_id=1, source_target_pairs={{0,4},{4,8},{8,12},{12,16},{16,20},{20,24},{24,28},{28,32},{32,36}... | collective-permute-start | bytes 786440 | tf_op jit(solution)/shard_map/ppermute | solution.py:241
  279.9 1.9 copy-start.8
  294.1 4.3 %collective-permute-start.18 = (bf16[16,64,128]{2,1,0:T(8,128)(2,1)}, bf16[16,64,128]{2,1,0:T(8,128)(2,1)S(1)}, u32[]{:S(2)}, u32[]{:S(2)}) collective-permute-start(bf16[16,64,128]{2,1,0:T(8,128)(2,1)} %get-tuple-element.134.refs_14_), channel_id=1, source_target_pairs={{0,252},{4,0},{8,4},{12,8},{16,12},{20,16},{24,20},{28,24},{32,28}... | collective-permute-start | bytes 786440 | tf_op jit(solution)/shard_map/ppermute | solution.py:243
  294.2 6.1 %collective-permute-start.17 = (bf16[16,64,128]{2,1,0:T(8,128)(2,1)}, bf16[16,64,128]{2,1,0:T(8,128)(2,1)S(1)}, u32[]{:S(2)}, u32[]{:S(2)}) collective-permute-start(bf16[16,64,128]{2,1,0:T(8,128)(2,1)} %get-tuple-element.134.refs_14_), channel_id=1, source_target_pairs={{0,4},{4,8},{8,12},{12,16},{16,20},{20,24},{24,28},{28,32},{32,36}... | collective-permute-start | bytes 786440 | tf_op jit(solution)/shard_map/ppermute | solution.py:241
  298.4 1.9 copy-start.5
  (3 other events, 2.1 us)
where the time goes:
time: 314 us; the launch traced here: 313 us
  waiting for transfers between devices  179 us (57%)
  Pallas kernels  66.7 us (21%)
  starting transfers between devices  42.1 us (13%)
  local copies, waits for them, and re-layouts  15.6 us (5%)
  other arithmetic  5.74 us (2%)
  between operations  3.36 us (1%)
    ppermute x2, waiting for transfers between devices, near(): lax.ppermute(packed, 'rhs', ring(count, -1))  89 us
    pallas_call x5, Pallas kernels, sweep(): pl.pallas_call(functools.partial(sweep_kernel, len(parts), half, chunk, a...  48.5 us
    all_to_all x1, waiting for transfers between devices, local_program(): lax.all_to_all(sent0, 'rows', split_axis=0, concat_axis=0, tiled=True)  34.6 us
    ppermute x2, waiting for transfers between devices, far(): lax.ppermute(below[half:], 'rhs', ring(count, -1))  22.4 us
    pallas_call x2, Pallas kernels, pack_blocks(): pl.pallas_call(pack_kernel, out_shape=jax.ShapeDtypeStruct((peers, width,...  14.1 us
    all_to_all x1, starting transfers between devices, local_program(): lax.all_to_all(send_codes.reshape(peers, 2), 'rows', split_axis=0, concat...  11.8 us
    ppermute x4, waiting for transfers between devices, neighbours(): lax.ppermute(rounded, 'rows', ring(count, -1))  11.1 us
    ppermute x2, waiting for transfers between devices, far(): lax.ppermute(above[:half], 'rhs', ring(count, 1))  9.62 us
  transfers between devices with their start and end apart: 22, of which 16 were waited for; matrix products, arithmetic and copies ran while one was open for 5% of the time, Pallas kernels for 6%

commit v1 on v0

--- a/solution.py
+++ b/solution.py
@@ -51,34 +51,6 @@
         ),
         name="form_blocks",
     )(owner, place, left, right, diag)
-
-
-def pack_kernel(order, count, got, packed, sems):
-    def begin(j, carry):
-        pltpu.make_async_copy(got.at[order[j]], packed.at[j], sems.at[j]).start()
-        return carry
-
-    def finish(j, carry):
-        pltpu.make_async_copy(got.at[0], packed.at[0], sems.at[j]).wait()
-        return carry
-
-    lax.fori_loop(0, count[0], begin, 0)
-    lax.fori_loop(0, count[0], finish, 0)
-
-
-def pack_blocks(got, order, count):
-    peers, width, _ = got.shape
-    return pl.pallas_call(
-        pack_kernel,
-        out_shape=jax.ShapeDtypeStruct((peers, width, width), jnp.bfloat16),
-        grid_spec=pltpu.PrefetchScalarGridSpec(
-            num_scalar_prefetch=2,
-            in_specs=[pl.BlockSpec(memory_space=pltpu.VMEM)],
-            out_specs=pl.BlockSpec(memory_space=pltpu.HBM),
-            scratch_shapes=[pltpu.SemaphoreType.DMA((peers,))],
-        ),
-        name="pack_blocks",
-    )(order, count, got)
 
 
 def read_bits(rows):
@@ -179,7 +151,7 @@
 
 
 def sweep(parts, counts, codes, coef, fields, acc_in=None, state=None, final=False):
-    half, width = parts[-1].shape[:2]
+    half, width = min(part.shape[0] for part in parts), parts[0].shape[1]
     chunk = min(CHUNK, half)
     held = sum(part.shape[0] for part in parts)
     rows, columns, _ = fields[1].shape
@@ -228,10 +200,9 @@
 
 def far(above, below):
     count = lax.axis_size("rhs")
-    half = above.shape[0] // 2
     return (
-        lax.ppermute(above[:half], "rhs", ring(count, 1)),
-        lax.ppermute(below[half:], "rhs", ring(count, -1)),
+        lax.ppermute(above, "rhs", ring(count, 1)),
+        lax.ppermute(below, "rhs", ring(count, -1)),
     )
 
 
@@ -270,27 +241,26 @@
     send_codes = jnp.sum(
         jnp.where(jnp.arange(2 * peers)[:, None] == spot[None, :], code[None, :], 0), axis=1
     )
+    sent0, sent1 = form_blocks(factor_left, factor_right, state_diag, dest, place, peers)
+    got0 = lax.all_to_all(sent0, "rows", split_axis=0, concat_axis=0, tiled=True)
+    near0 = near(got0)
+    half = peers // 2
+    far0 = far(near0[0][:half], near0[1][half:])
+    send_codes, _ = lax.optimization_barrier((send_codes, got0))
     got_codes = lax.all_to_all(
         send_codes.reshape(peers, 2), "rows", split_axis=0, concat_axis=0, tiled=True
     ).T
-    number = jnp.arange(peers)
-    key = jnp.where(got_codes > 0, got_codes, jnp.int32(1 << 20))
-    ahead = (key[:, None, :] < key[:, :, None]) | (
-        (key[:, None, :] == key[:, :, None]) & (number[None, None, :] < number[None, :, None])
-    )
-    rank = jnp.sum(ahead.astype(jnp.int32), axis=2)
-    chosen = rank[:, None, :] == number[None, :, None]
-    source = jnp.sum(jnp.where(chosen, number[None, None, :], 0), axis=2)
-    sorted_codes = jnp.sum(jnp.where(chosen, got_codes[:, None, :], 0), axis=2)
-    count = jnp.sum((got_codes > 0).astype(jnp.int32), axis=1)
-
-    up = lax.ppermute(sorted_codes, "rhs", ring(across, 1))
-    down = lax.ppermute(sorted_codes, "rhs", ring(across, -1))
-    far_codes = lax.ppermute(sorted_codes, "rhs", ring(across, 2))
-    all_codes = jnp.stack([sorted_codes, up, down, far_codes], axis=1)
-    all_codes = all_codes.reshape(2, 4, 2, peers // 2)
-    all_counts = jnp.sum((all_codes > 0).astype(jnp.int32), axis=3).reshape(2, 8)
+    sent1, got_codes = lax.optimization_barrier((sent1, got_codes))
+    got1 = lax.all_to_all(sent1, "rows", split_axis=0, concat_axis=0, tiled=True)
+
+    up = lax.ppermute(got_codes, "rhs", ring(across, 1))
+    down = lax.ppermute(got_codes, "rhs", ring(across, -1))
+    far_codes = lax.ppermute(got_codes, "rhs", ring(across, 2))
+    all_codes = jnp.stack([got_codes, up, down, far_codes], axis=1)
+    all_codes = all_codes.reshape(2, 4, 2, half)
+    all_counts = half * jnp.any(all_codes > 0, axis=3).astype(jnp.int32).reshape(2, 8)
     all_codes = all_codes.reshape(2, 4 * peers)
+
     low = low_bound[0]
     high = high_bound[0]
     theta = (high + low) / 2.0
@@ -298,13 +268,11 @@
     sigma = theta / delta
     rho = 1.0 / sigma
     coefs = []
-    for number in range(ITERS):
+    for _ in range(ITERS):
         rho_next = 1.0 / (2.0 * sigma - rho)
         coefs.append(jnp.stack([rho_next * rho, 2.0 * rho_next / delta]))
         rho = rho_next
     tables = (
-        source[1],
-        count[1:],
         all_counts[0],
         all_counts[1],
         all_counts.reshape(16),
@@ -314,15 +282,8 @@
         *coefs,
     )
 
-    sent0, sent1 = form_blocks(factor_left, factor_right, state_diag, dest, place, peers)
-    got0 = lax.all_to_all(sent0, "rows", split_axis=0, concat_axis=0, tiled=True)
-    packed0 = pack_blocks(got0, source[0], count[:1])
-    near0 = near(packed0)
-    far0 = far(*near0)
-    sent1, _, *tables = lax.optimization_barrier((sent1, packed0, *tables))
-    order1, number1, counts0, counts1, counts, codes0, codes1, codes, *coefs = tables
-    got1 = lax.all_to_all(sent1, "rows", split_axis=0, concat_axis=0, tiled=True)
-    packed1 = pack_blocks(got1, order1, number1)
+    got1, *tables = lax.optimization_barrier((got1, *tables))
+    counts0, counts1, counts, codes0, codes1, codes, *coefs = tables
 
     residual = rhs_in
     direction = residual / theta
@@ -333,17 +294,22 @@
         (acc,) = sweep(parts, counts0, codes0, coefs[0], fields)
         return acc
 
-    def with_second(parts, packed):
-        near1 = near(packed)
+    def with_second(parts, got):
+        first, second = got[:half], got[half:]
+        up_first = lax.ppermute(first, "rhs", ring(across, 1))
+        down_second = lax.ppermute(second, "rhs", ring(across, -1))
+        up_second = lax.ppermute(second, "rhs", ring(across, 1))
+        down_first = lax.ppermute(first, "rhs", ring(across, -1))
         acc = first_product(parts)
-        return acc, [packed, *near1, *far(*near1)]
-
-    def without_second(parts, packed):
-        half = packed.shape[0] // 2
-        return first_product(parts), [packed, packed, packed, packed[:half], packed[half:]]
-
-    parts0 = [packed0, *near0, *far0]
-    acc, parts1 = lax.cond(jnp.sum(counts1) > 0, with_second, without_second, parts0, packed1)
+        far1 = far(up_first, down_second)
+        return acc, [up_first, up_second, down_first, down_second, *far1]
+
+    def without_second(parts, got):
+        return first_product(parts), [jnp.zeros(got[:half].shape, got.dtype)] * 6
+
+    parts0 = [got0, *near0, *far0]
+    acc, others1 = lax.cond(jnp.sum(counts1) > 0, with_second, without_second, parts0, got1)
+    parts1 = [got1, *others1]
     for number in range(ITERS):
         state = (adjoint, residual, direction)
         final = number + 1 == ITERS

time: 314 us -> 311 us (level)
  the two profiles are of different devices: /device:TPU:32 before, /device:TPU:33 now
where the time goes in v1:
time: 311 us
  waiting for transfers between devices  183 us (59%)
  Pallas kernels  48.7 us (16%)
  starting transfers between devices  42.5 us (14%)
  blocking collectives  15.2 us (5%)
  local copies, waits for them, and re-layouts  11.9 us (4%)
  other arithmetic  5.6 us (2%)
  between operations  3.37 us (1%)
    all_to_all x1, waiting for transfers between devices, local_program(): lax.all_to_all(sent0, 'rows', split_axis=0, concat_axis=0, tiled=True)  49.8 us
    pallas_call x5, Pallas kernels, sweep(): pl.pallas_call(functools.partial(sweep_kernel, len(parts), half, chunk, a...  44.6 us
    ppermute x1, waiting for transfers between devices, near(): lax.ppermute(packed, 'rhs', ring(count, -1))  43.3 us
    ppermute x2, waiting for transfers between devices, far(): lax.ppermute(below, 'rhs', ring(count, -1))  21.3 us
    ppermute x1, waiting for transfers between devices, with_second(): down_second = lax.ppermute(second, 'rhs', ring(across, -1))  20.3 us
    ppermute x1, waiting for transfers between devices, with_second(): up_second = lax.ppermute(second, 'rhs', ring(across, 1))  16.9 us
    ppermute x1, waiting for transfers between devices, local_program(): far_codes = lax.ppermute(got_codes, 'rhs', ring(across, 2))  16.3 us
    all_to_all x1, blocking collectives, local_program(): lax.all_to_all(send_codes.reshape(peers, 2), 'rows', split_axis=0, concat...  15.2 us
  transfers between devices with their start and end apart: 23, of which 11 were waited for; matrix products, arithmetic and copies ran while one was open for 3% of the time, Pallas kernels for 2%

profile of v1, /device:TPU:33, one launch (start us, length us, event | category | flops | bytes accessed | tf_op | source)
XLA Modules:
  0.0 310.8 jit_solution(14212140236706499043)
XLA Ops:
  0.6 1.4 convert_reduce_fusion.place
  2.1 4.1 %form_blocks.1 = (bf16[64,128,128]{2,1,0:T(8,128)(2,1)}, bf16[64,128,128]{2,1,0:T(8,128)(2,1)}) custom-call(s32[32]{0:T(128)} %bitcast.30, s32[32]{0:T(128)} %convert_reduce_fusion.place, bf16[32,128,128]{2,1,0:T(8,128)(2,1)} %left.1, bf16[32,128,128]{2,1,0:T(8,128)(2,1)} %right.1, f32[32,128]{1,0:T(8,128)} %diag.1), custom_call_target="tpu_custom_call" | custom-call | tf_op jit(solution)/shard_map/form_blocks/pallas_call | solution.py:40
  6.2 12.2 %all-to-all-start = ((bf16[64,128,128]{2,1,0:T(8,128)(2,1)}), bf16[64,128,128]{2,1,0:T(8,128)(2,1)S(1)}, u32[]{:S(2)}, u32[]{:S(2)}) async-start(bf16[64,128,128]{2,1,0:T(8,128)(2,1)} %get-tuple-element.107), calls=%async_computation | async-start | bytes 4194304 | tf_op jit(solution)/shard_map/all_to_all | solution.py:245
  18.6 49.8 %all-to-all-done.refs_3_ = bf16[64,128,128]{2,1,0:T(8,128)(2,1)S(1)} async-done(((bf16[64,128,128]{2,1,0:T(8,128)(2,1)}), bf16[64,128,128]{2,1,0:T(8,128)(2,1)S(1)}, u32[]{:S(2)}, u32[]{:S(2)}) %all-to-all-start) | async-done | bytes 2097184 | tf_op jit(solution)/shard_map/all_to_all | solution.py:245
  68.5 15.2 %all_to_all.22 = s32[64,1,2]{2,1,0:T(1,128)S(1)} all-to-all(s32[64,1,2]{2,1,0:T(1,128)S(1)} %bitcast.20), channel_id=1, replica_groups=mesh['rows'=64,'rhs'=4] {'rows'}, dimensions={0} | all-to-all | bytes 1024 | tf_op jit(solution)/shard_map/all_to_all | solution.py:250
  83.8 6.6 %all-to-all-start.2 = ((bf16[64,128,128]{2,1,0:T(8,128)(2,1)}), bf16[64,128,128]{2,1,0:T(8,128)(2,1)}, u32[]{:S(2)}, u32[]{:S(2)}) async-start(bf16[64,128,128]{2,1,0:T(8,128)(2,1)} %get-tuple-element.109), calls=%async_computation.2 | async-start | bytes 4194304 | tf_op jit(solution)/shard_map/all_to_all | solution.py:254
  90.4 2.6 collective-permute-start.10
  94.3 43.3 %collective-permute-done.10.refs_5_ = bf16[64,128,128]{2,1,0:T(8,128)(2,1)S(1)} collective-permute-done((bf16[64,128,128]{2,1,0:T(8,128)(2,1)S(1)}, bf16[64,128,128]{2,1,0:T(8,128)(2,1)S(1)}, u32[]{:S(2)}, u32[]{:S(2)}) %collective-permute-start.10) | collective-permute-done | bytes 2097184 | tf_op jit(solution)/shard_map/ppermute | solution.py:197
  138.7 3.5 %collective-permute-start.12 = (bf16[32,128,128]{2,1,0:T(8,128)(2,1)}, bf16[32,128,128]{2,1,0:T(8,128)(2,1)S(1)}, u32[]{:S(2)}, u32[]{:S(2)}) collective-permute-start(bf16[32,128,128]{2,1,0:T(8,128)(2,1)} %slice.39), channel_id=1, source_target_pairs={{0,3},{1,0},{2,1},{3,2},{4,7},{5,4},{6,5},{7,6},{8,11},{9,8},{10,9... | collective-permute-start | bytes 3145736 | tf_op jit(solution)/shard_map/ppermute | solution.py:205
  142.2 1.4 copy-done.1
  145.7 1.9 fusion.1
  148.8 1.5 collective-permute-start.7
  151.6 16.3 %collective-permute-done.8 = s32[2,64]{1,0:T(2,128)S(1)} collective-permute-done((s32[2,64]{1,0:T(2,128)S(1)}, s32[2,64]{1,0:T(2,128)S(1)}, u32[]{:S(2)}, u32[]{:S(2)}) %collective-permute-start.8) | collective-permute-done | bytes 544 | tf_op jit(solution)/shard_map/ppermute | solution.py:258
  167.9 2.3 collective-permute-start.14
  175.6 74.0 %conditional.1 = (f32[16,64,128]{2,1,0:T(8,128)S(1)}, bf16[32,128,128]{2,1,0:T(8,128)(2,1)}, bf16[32,128,128]{2,1,0:T(8,128)(2,1)}, bf16[32,128,128]{2,1,0:T(8,1...) conditional(s32[]{:T(128)} %convert_element_type.13, ...), branch_computations={%region_4.5_spmd, %region_5.6_spmd} | conditional | bytes 29360424 | solution.py:311
  175.8 3.2 %fusion.2 = (bf16[32,128,128]{2,1,0:T(8,128)(2,1)}, bf16[32,128,128]{2,1,0:T(8,128)(2,1)}) fusion(bf16[64,128,128]{2,1,0:T(8,128)(2,1)} %get-tuple-element.68), kind=kLoop, calls=%fused_computation.20 | loop fusion | bytes 4194304 | tf_op jit(solution)/shard_map/cond/branch_1_fun/slice | solution.py:298
  179.0 1.5 collective-permute-start
  180.5 2.7 collective-permute-start.2
  183.2 20.3 %collective-permute-done.3 = bf16[32,128,128]{2,1,0:T(8,128)(2,1)} collective-permute-done((bf16[32,128,128]{2,1,0:T(8,128)(2,1)}, bf16[32,128,128]{2,1,0:T(8,128)(2,1)}, u32[]{:S(2)}, u32[]{:S(2)}) %collective-permute-start.3) | collective-permute-done | bytes 1048608 | tf_op jit(solution)/shard_map/cond/branch_1_fun/ppermute | solution.py:300
  203.5 1.5 collective-permute-start.5
  205.0 5.2 %sweep.7 = f32[16,64,128]{2,1,0:T(8,128)S(1)} custom-call(s32[8]{0:T(128)S(1)} %get-tuple-element.57.refs_0_, s32[256]{0:T(256)S(1)} %get-tuple-element.58.refs_1_, f32[2]{0:T(128)S(1)} %get-tuple-element.59.refs_2_, bf16[64,128,128]{2,1,0:T(8,128)(2,1)S(1)} %get-tuple-element.60.refs_3_, bf16[64,128,128]{2,1,0:T(8,128)(2,1)} %get-tuple-element.61.refs_4_, ...), custom_call_target="tpu_custom_call" | custom-call | tf_op jit(solution)/shard_map/cond/branch_1_fun/sweep/pallas_call | solution.py:167
  210.2 16.9 %collective-permute-done.1 = bf16[32,128,128]{2,1,0:T(8,128)(2,1)} collective-permute-done((bf16[32,128,128]{2,1,0:T(8,128)(2,1)}, bf16[32,128,128]{2,1,0:T(8,128)(2,1)}, u32[]{:S(2)}, u32[]{:S(2)}) %collective-permute-start.1) | collective-permute-done | bytes 1048608 | tf_op jit(solution)/shard_map/cond/branch_1_fun/ppermute | solution.py:301
  227.2 21.3 %collective-permute-done.5 = bf16[32,128,128]{2,1,0:T(8,128)(2,1)} collective-permute-done((bf16[32,128,128]{2,1,0:T(8,128)(2,1)}, bf16[32,128,128]{2,1,0:T(8,128)(2,1)}, u32[]{:S(2)}, u32[]{:S(2)}) %collective-permute-start.5) | collective-permute-done | bytes 1048608 | tf_op jit(solution)/shard_map/cond/branch_1_fun/ppermute | solution.py:205
  248.5 1.2 collective-permute-done.4
  249.7 8.9 %sweep.8 = (bf16[16,64,128]{2,1,0:T(8,128)(2,1)}, f32[16,64,128]{2,1,0:T(8,128)}, f32[16,64,128]{2,1,0:T(8,128)}, f32[16,64,128]{2,1,0:T(8,128)}) custom-call(s32[8]{0:T(128)} %copy-done.8, s32[256]{0:T(256)} %squeeze.21.refs_1_, f32[2]{0:T(128)S(1)} %get-tuple-element.118.refs_2_, bf16[64,128,128]{2,1,0:T(8,128)(2,1)} %all-to-all-done.2.refs_3_.refs_8_, ...), custom_call_target="tpu_custom_call" | custom-call | tf_op jit(solution)/shard_map/sweep/pallas_call | solution.py:167
  258.5 1.5 collective-permute-start.16
  260.4 4.6 %collective-permute-done.16.refs_17_ = bf16[16,64,128]{2,1,0:T(8,128)(2,1)S(1)} collective-permute-done((bf16[16,64,128]{2,1,0:T(8,128)(2,1)}, bf16[16,64,128]{2,1,0:T(8,128)(2,1)S(1)}, u32[]{:S(2)}, u32[]{:S(2)}) %collective-permute-start.16) | collective-permute-done | bytes 262176 | tf_op jit(solution)/shard_map/ppermute | solution.py:214
  265.7 10.3 %sweep.9 = (bf16[16,64,128]{2,1,0:T(8,128)(2,1)}, f32[16,64,128]{2,1,0:T(8,128)}, f32[16,64,128]{2,1,0:T(8,128)}, f32[16,64,128]{2,1,0:T(8,128)}) custom-call(s32[16]{0:T(128)} %mul.57.refs_0_, s32[512]{0:T(512)} %reshape_reshape_reshape.3.refs_1_, f32[2]{0:T(128)} %get-tuple-element.126.refs_2_, bf16[64,128,128]{2,1,0:T(8,128)(2,1)S(1)} %all-to-all-done.refs_3_, ...), custom_call_target="tpu_custom_call" | custom-call | tf_op jit(solution)/shard_map/sweep/pallas_call | solution.py:167
  277.8 4.6 %collective-permute-done.18.refs_17_ = bf16[16,64,128]{2,1,0:T(8,128)(2,1)S(1)} collective-permute-done((bf16[16,64,128]{2,1,0:T(8,128)(2,1)}, bf16[16,64,128]{2,1,0:T(8,128)(2,1)S(1)}, u32[]{:S(2)}, u32[]{:S(2)}) %collective-permute-start.18) | collective-permute-done | bytes 262176 | tf_op jit(solution)/shard_map/ppermute | solution.py:214
  283.2 10.3 %sweep.10 = (bf16[16,64,128]{2,1,0:T(8,128)(2,1)}, f32[16,64,128]{2,1,0:T(8,128)}, f32[16,64,128]{2,1,0:T(8,128)}, f32[16,64,128]{2,1,0:T(8,128)}) custom-call(s32[16]{0:T(128)} %mul.57.refs_0_, s32[512]{0:T(512)} %reshape_reshape_reshape.3.refs_1_, f32[2]{0:T(128)} %get-tuple-element.125.refs_2_, bf16[64,128,128]{2,1,0:T(8,128)(2,1)S(1)} %all-to-all-done.refs_3_, ...), custom_call_target="tpu_custom_call" | custom-call | tf_op jit(solution)/shard_map/sweep/pallas_call | solution.py:167
  295.3 4.6 %collective-permute-done.20.refs_17_ = bf16[16,64,128]{2,1,0:T(8,128)(2,1)S(1)} collective-permute-done((bf16[16,64,128]{2,1,0:T(8,128)(2,1)}, bf16[16,64,128]{2,1,0:T(8,128)(2,1)S(1)}, u32[]{:S(2)}, u32[]{:S(2)}) %collective-permute-start.20) | collective-permute-done | bytes 262176 | tf_op jit(solution)/shard_map/ppermute | solution.py:214
  300.7 10.0 %sweep.11 = (f32[16,64,128]{2,1,0:T(8,128)}, f32[16,64,128]{2,1,0:T(8,128)}) custom-call(s32[16]{0:T(128)} %mul.57.refs_0_, s32[512]{0:T(512)} %reshape_reshape_reshape.3.refs_1_, f32[2]{0:T(128)} %get-tuple-element.113.refs_2_, bf16[64,128,128]{2,1,0:T(8,128)(2,1)S(1)} %all-to-all-done.refs_3_, bf16[64,128,128]{2,1,0:T(8,128)(2,1)} %copy-done.1, ...), custom_call_target="tpu_custom_call" | custom-call | tf_op jit(solution)/shard_map/sweep/pallas_call | solution.py:167
  (79 shorter events, 16.9 us)
Async XLA Ops:
  6.2 12.2 %copy-start.9 = (s32[32,1]{0,1:T(1,128)S(1)}, s32[32,1]{0,1:T(1,128)}, u32[]{:S(2)}) copy-start(s32[32,1]{0,1:T(1,128)} %param.15) | copy-start | bytes 388
  6.2 12.2 %copy-start.10 = (s32[32]{0:T(128)S(1)}, s32[32]{0:T(128)}, u32[]{:S(2)}) copy-start(s32[32]{0:T(128)} %convert_reduce_fusion.place) | copy-start | bytes 388
  6.2 12.2 %copy-start.11 = (s32[32]{0:T(128)S(1)}, s32[32]{0:T(128)}, u32[]{:S(2)}) copy-start(s32[32]{0:T(128)} %param.18) | copy-start | bytes 388
  6.2 12.2 %copy-start.12 = (s32[32]{0:T(128)S(1)}, s32[32]{0:T(128)}, u32[]{:S(2)}) copy-start(s32[32]{0:T(128)} %param.17) | copy-start | bytes 388
  6.2 12.2 %copy-start.13 = (s32[32]{0:T(128)S(1)}, s32[32]{0:T(128)}, u32[]{:S(2)}) copy-start(s32[32]{0:T(128)} %param.16) | copy-start | bytes 388
  6.2 62.1 %all-to-all-start = ((bf16[64,128,128]{2,1,0:T(8,128)(2,1)}), bf16[64,128,128]{2,1,0:T(8,128)(2,1)S(1)}, u32[]{:S(2)}, u32[]{:S(2)}) async-start(bf16[64,128,128]{2,1,0:T(8,128)(2,1)} %get-tuple-element.107), calls=%async_computation | async-start | bytes 4194304 | tf_op jit(solution)/shard_map/all_to_all | solution.py:245
  83.8 90.1 %all-to-all-start.2 = ((bf16[64,128,128]{2,1,0:T(8,128)(2,1)}), bf16[64,128,128]{2,1,0:T(8,128)(2,1)}, u32[]{:S(2)}, u32[]{:S(2)}) async-start(bf16[64,128,128]{2,1,0:T(8,128)(2,1)} %get-tuple-element.109), calls=%async_computation.2 | async-start | bytes 4194304 | tf_op jit(solution)/shard_map/all_to_all | solution.py:254
  90.4 47.2 %collective-permute-start.10 = (bf16[64,128,128]{2,1,0:T(8,128)(2,1)S(1)}, bf16[64,128,128]{2,1,0:T(8,128)(2,1)S(1)}, u32[]{:S(2)}, u32[]{:S(2)}) collective-permute-start(bf16[64,128,128]{2,1,0:T(8,128)(2,1)S(1)} %all-to-all-done.refs_3_), channel_id=1, source_target_pairs={{0,3},{1,0},{2,1},{3,2},{4,7},{5,4},{6,5},{7,6},{8,11},{9,8},{10,9... | collective-permute-start | bytes 6291464 | tf_op jit(solution)/shard_map/ppermute | solution.py:197
  93.0 49.3 %collective-permute-start.9 = (bf16[64,128,128]{2,1,0:T(8,128)(2,1)S(1)}, bf16[64,128,128]{2,1,0:T(8,128)(2,1)S(1)}, u32[]{:S(2)}, u32[]{:S(2)}) collective-permute-start(bf16[64,128,128]{2,1,0:T(8,128)(2,1)S(1)} %all-to-all-done.refs_3_), channel_id=1, source_target_pairs={{0,1},{1,2},{2,3},{3,0},{4,5},{5,6},{6,7},{7,4},{8,9},{9,10},{10,1... | collective-permute-start | bytes 6291464 | tf_op jit(solution)/shard_map/ppermute | solution.py:196
  137.6 7.1 %copy-start = (bf16[64,128,128]{2,1,0:T(8,128)(2,1)}, bf16[64,128,128]{2,1,0:T(8,128)(2,1)S(1)}, u32[]{:S(2)}) copy-start(bf16[64,128,128]{2,1,0:T(8,128)(2,1)S(1)} %collective-permute-done.10.refs_5_) | copy-start | bytes 6291460
  138.7 36.9 %collective-permute-start.12 = (bf16[32,128,128]{2,1,0:T(8,128)(2,1)}, bf16[32,128,128]{2,1,0:T(8,128)(2,1)S(1)}, u32[]{:S(2)}, u32[]{:S(2)}) collective-permute-start(bf16[32,128,128]{2,1,0:T(8,128)(2,1)} %slice.39), channel_id=1, source_target_pairs={{0,3},{1,0},{2,1},{3,2},{4,7},{5,4},{6,5},{7,6},{8,11},{9,8},{10,9... | collective-permute-start | bytes 3145736 | tf_op jit(solution)/shard_map/ppermute | solution.py:205
  142.2 1.4 copy-start.1
  144.7 31.0 %collective-permute-start.11 = (bf16[32,128,128]{2,1,0:T(8,128)(2,1)}, bf16[32,128,128]{2,1,0:T(8,128)(2,1)}, u32[]{:S(2)}, u32[]{:S(2)}) collective-permute-start(bf16[32,128,128]{2,1,0:T(8,128)(2,1)} %slice.38), channel_id=1, source_target_pairs={{0,1},{1,2},{2,3},{3,0},{4,5},{5,6},{6,7},{7,4},{8,9},{9,10},{10,1... | collective-permute-start | bytes 3145736 | tf_op jit(solution)/shard_map/ppermute | solution.py:204
  147.6 20.3 %collective-permute-start.8 = (s32[2,64]{1,0:T(2,128)S(1)}, s32[2,64]{1,0:T(2,128)S(1)}, u32[]{:S(2)}, u32[]{:S(2)}) collective-permute-start(s32[2,64]{1,0:T(2,128)S(1)} %bitcast.21), channel_id=1, source_target_pairs={{0,2},{1,3},{2,0},{3,1},{4,6},{5,7},{6,4},{7,5},{8,10},{9,11},{10,... | collective-permute-start | bytes 1544 | tf_op jit(solution)/shard_map/ppermute | solution.py:258
  148.8 21.5 %collective-permute-start.7 = (s32[2,64]{1,0:T(2,128)S(1)}, s32[2,64]{1,0:T(2,128)S(1)}, u32[]{:S(2)}, u32[]{:S(2)}) collective-permute-start(s32[2,64]{1,0:T(2,128)S(1)} %bitcast.22), channel_id=1, source_target_pairs={{0,3},{1,0},{2,1},{3,2},{4,7},{5,4},{6,5},{7,6},{8,11},{9,8},{10,9... | collective-permute-start | bytes 1544 | tf_op jit(solution)/shard_map/ppermute | solution.py:257
  150.3 21.0 %collective-permute-start.6 = (s32[2,64]{1,0:T(2,128)S(1)}, s32[2,64]{1,0:T(2,128)S(1)}, u32[]{:S(2)}, u32[]{:S(2)}) collective-permute-start(s32[2,64]{1,0:T(2,128)S(1)} %bitcast.23), channel_id=1, source_target_pairs={{0,1},{1,2},{2,3},{3,0},{4,5},{5,6},{6,7},{7,4},{8,9},{9,10},{10,1... | collective-permute-start | bytes 1544 | tf_op jit(solution)/shard_map/ppermute | solution.py:256
  167.9 7.7 %collective-permute-start.14 = (bf16[16,64,128]{2,1,0:T(8,128)(2,1)S(1)}, bf16[16,64,128]{2,1,0:T(8,128)(2,1)}, u32[]{:S(2)}, u32[]{:S(2)}) collective-permute-start(bf16[16,64,128]{2,1,0:T(8,128)(2,1)S(1)} %get-tuple-element.145.refs_11_), channel_id=1, source_target_pairs={{0,252},{4,0},{8,4},{12,8},{16,12},{20,16},{24,20},{28,24},{32,28}... | collective-permute-start | bytes 786440 | tf_op jit(solution)/shard_map/ppermute | solution.py:214
  170.3 5.3 %collective-permute-start.13 = (bf16[16,64,128]{2,1,0:T(8,128)(2,1)S(1)}, bf16[16,64,128]{2,1,0:T(8,128)(2,1)}, u32[]{:S(2)}, u32[]{:S(2)}) collective-permute-start(bf16[16,64,128]{2,1,0:T(8,128)(2,1)S(1)} %get-tuple-element.145.refs_11_), channel_id=1, source_target_pairs={{0,4},{4,8},{8,12},{12,16},{16,20},{20,24},{24,28},{28,32},{32,36}... | collective-permute-start | bytes 786440 | tf_op jit(solution)/shard_map/ppermute | solution.py:212
  172.4 3.3 %copy-start.8 = (s32[8]{0:T(128)}, s32[8]{0:T(128)S(1)}, u32[]{:S(2)}) copy-start(s32[8]{0:T(128)S(1)} %squeeze.19.refs_0_) | copy-start | bytes 100
  179.0 24.5 %collective-permute-start.3 = (bf16[32,128,128]{2,1,0:T(8,128)(2,1)}, bf16[32,128,128]{2,1,0:T(8,128)(2,1)}, u32[]{:S(2)}, u32[]{:S(2)}) collective-permute-start(bf16[32,128,128]{2,1,0:T(8,128)(2,1)} %get-tuple-element.147), channel_id=1, source_target_pairs={{0,3},{1,0},{2,1},{3,2},{4,7},{5,4},{6,5},{7,6},{8,11},{9,8},{10,9... | collective-permute-start | bytes 3145736 | tf_op jit(solution)/shard_map/cond/branch_1_fun/ppermute | solution.py:300
  179.0 26.0 %collective-permute-start = (bf16[32,128,128]{2,1,0:T(8,128)(2,1)}, bf16[32,128,128]{2,1,0:T(8,128)(2,1)}, u32[]{:S(2)}, u32[]{:S(2)}) collective-permute-start(bf16[32,128,128]{2,1,0:T(8,128)(2,1)} %get-tuple-element.148), channel_id=1, source_target_pairs={{0,1},{1,2},{2,3},{3,0},{4,5},{5,6},{6,7},{7,4},{8,9},{9,10},{10,1... | collective-permute-start | bytes 3145736 | tf_op jit(solution)/shard_map/cond/branch_1_fun/ppermute | solution.py:299
  180.5 46.7 %collective-permute-start.1 = (bf16[32,128,128]{2,1,0:T(8,128)(2,1)}, bf16[32,128,128]{2,1,0:T(8,128)(2,1)}, u32[]{:S(2)}, u32[]{:S(2)}) collective-permute-start(bf16[32,128,128]{2,1,0:T(8,128)(2,1)} %get-tuple-element.147), channel_id=1, source_target_pairs={{0,1},{1,2},{2,3},{3,0},{4,5},{5,6},{6,7},{7,4},{8,9},{9,10},{10,1... | collective-permute-start | bytes 3145736 | tf_op jit(solution)/shard_map/cond/branch_1_fun/ppermute | solution.py:301
  180.5 46.7 %collective-permute-start.2 = (bf16[32,128,128]{2,1,0:T(8,128)(2,1)}, bf16[32,128,128]{2,1,0:T(8,128)(2,1)}, u32[]{:S(2)}, u32[]{:S(2)}) collective-permute-start(bf16[32,128,128]{2,1,0:T(8,128)(2,1)} %get-tuple-element.148), channel_id=1, source_target_pairs={{0,3},{1,0},{2,1},{3,2},{4,7},{5,4},{6,5},{7,6},{8,11},{9,8},{10,9... | collective-permute-start | bytes 3145736 | tf_op jit(solution)/shard_map/cond/branch_1_fun/ppermute | solution.py:302
  203.5 44.9 %collective-permute-start.5 = (bf16[32,128,128]{2,1,0:T(8,128)(2,1)}, bf16[32,128,128]{2,1,0:T(8,128)(2,1)}, u32[]{:S(2)}, u32[]{:S(2)}) collective-permute-start(bf16[32,128,128]{2,1,0:T(8,128)(2,1)} %collective-permute-done.3), channel_id=1, source_target_pairs={{0,3},{1,0},{2,1},{3,2},{4,7},{5,4},{6,5},{7,6},{8,11},{9,8},{10,9... | collective-permute-start | bytes 3145736 | tf_op jit(solution)/shard_map/cond/branch_1_fun/ppermute | solution.py:205
  205.0 44.7 %collective-permute-start.4 = (bf16[32,128,128]{2,1,0:T(8,128)(2,1)}, bf16[32,128,128]{2,1,0:T(8,128)(2,1)}, u32[]{:S(2)}, u32[]{:S(2)}) collective-permute-start(bf16[32,128,128]{2,1,0:T(8,128)(2,1)} %collective-permute-done), channel_id=1, source_target_pairs={{0,1},{1,2},{2,3},{3,0},{4,5},{5,6},{6,7},{7,4},{8,9},{9,10},{10,1... | collective-permute-start | bytes 3145736 | tf_op jit(solution)/shard_map/cond/branch_1_fun/ppermute | solution.py:204
  258.5 6.4 %collective-permute-start.16 = (bf16[16,64,128]{2,1,0:T(8,128)(2,1)}, bf16[16,64,128]{2,1,0:T(8,128)(2,1)S(1)}, u32[]{:S(2)}, u32[]{:S(2)}) collective-permute-start(bf16[16,64,128]{2,1,0:T(8,128)(2,1)} %get-tuple-element.129.refs_16_), channel_id=1, source_target_pairs={{0,252},{4,0},{8,4},{12,8},{16,12},{20,16},{24,20},{28,24},{32,28}... | collective-permute-start | bytes 786440 | tf_op jit(solution)/shard_map/ppermute | solution.py:214
  260.0 4.9 %collective-permute-start.15 = (bf16[16,64,128]{2,1,0:T(8,128)(2,1)}, bf16[16,64,128]{2,1,0:T(8,128)(2,1)S(1)}, u32[]{:S(2)}, u32[]{:S(2)}) collective-permute-start(bf16[16,64,128]{2,1,0:T(8,128)(2,1)} %get-tuple-element.129.refs_16_), channel_id=1, source_target_pairs={{0,4},{4,8},{8,12},{12,16},{16,20},{20,24},{24,28},{28,32},{32,36}... | collective-permute-start | bytes 786440 | tf_op jit(solution)/shard_map/ppermute | solution.py:212
  276.0 6.4 %collective-permute-start.18 = (bf16[16,64,128]{2,1,0:T(8,128)(2,1)}, bf16[16,64,128]{2,1,0:T(8,128)(2,1)S(1)}, u32[]{:S(2)}, u32[]{:S(2)}) collective-permute-start(bf16[16,64,128]{2,1,0:T(8,128)(2,1)} %get-tuple-element.133.refs_16_), channel_id=1, source_target_pairs={{0,252},{4,0},{8,4},{12,8},{16,12},{20,16},{24,20},{28,24},{32,28}... | collective-permute-start | bytes 786440 | tf_op jit(solution)/shard_map/ppermute | solution.py:214
  277.2 5.2 %collective-permute-start.17 = (bf16[16,64,128]{2,1,0:T(8,128)(2,1)}, bf16[16,64,128]{2,1,0:T(8,128)(2,1)S(1)}, u32[]{:S(2)}, u32[]{:S(2)}) collective-permute-start(bf16[16,64,128]{2,1,0:T(8,128)(2,1)} %get-tuple-element.133.refs_16_), channel_id=1, source_target_pairs={{0,4},{4,8},{8,12},{12,16},{16,20},{20,24},{24,28},{28,32},{32,36}... | collective-permute-start | bytes 786440 | tf_op jit(solution)/shard_map/ppermute | solution.py:212
  293.4 6.4 %collective-permute-start.20 = (bf16[16,64,128]{2,1,0:T(8,128)(2,1)}, bf16[16,64,128]{2,1,0:T(8,128)(2,1)S(1)}, u32[]{:S(2)}, u32[]{:S(2)}) collective-permute-start(bf16[16,64,128]{2,1,0:T(8,128)(2,1)} %get-tuple-element.137.refs_16_), channel_id=1, source_target_pairs={{0,252},{4,0},{8,4},{12,8},{16,12},{20,16},{24,20},{28,24},{32,28}... | collective-permute-start | bytes 786440 | tf_op jit(solution)/shard_map/ppermute | solution.py:214
  294.3 5.5 %collective-permute-start.19 = (bf16[16,64,128]{2,1,0:T(8,128)(2,1)}, bf16[16,64,128]{2,1,0:T(8,128)(2,1)S(1)}, u32[]{:S(2)}, u32[]{:S(2)}) collective-permute-start(bf16[16,64,128]{2,1,0:T(8,128)(2,1)} %get-tuple-element.137.refs_16_), channel_id=1, source_target_pairs={{0,4},{4,8},{8,12},{12,16},{16,20},{20,24},{24,28},{28,32},{32,36}... | collective-permute-start | bytes 786440 | tf_op jit(solution)/shard_map/ppermute | solution.py:212
  299.8 0.8 copy-start.3
  (5 other events, 3.7 us)

commit v2 on v1

--- a/solution.py
+++ b/solution.py
@@ -8,7 +8,6 @@
 from jax.sharding import PartitionSpec as P
 
 ITERS = 4
-CHUNK = 32
 
 
 def form_kernel(owner, place, left, right, diag, out0, out1, held, sems):
@@ -57,7 +56,7 @@
     return (3 * rows - 1).bit_length()
 
 
-def sweep_kernel(num_parts, half, chunk, has_acc, last, final, *refs):
+def sweep_kernel(num_parts, half, has_acc, last, final, *refs):
     counts, codes, coef = refs[:3]
     refs = refs[3:]
     parts, refs = refs[:num_parts], refs[num_parts:]
@@ -68,7 +67,7 @@
     outs, refs = refs[:num_outs], refs[num_outs:]
     ext, acc, held, kept, rounded, sems, field_sems, state_sems, out_sems = refs
     rows = fields[1].shape[0]
-    steps = half // chunk
+    group = 2 * half
     halves = [(part, i) for part in parts for i in range(0, part.shape[0], half)]
     bits = read_bits(rows)
     field_copies = [
@@ -78,15 +77,12 @@
     for copy in field_copies:
         copy.start()
     for a, (part, first) in enumerate(halves):
-        for c in range(steps):
-
-            @pl.when(counts[a] > c * chunk)
-            def _():
-                pltpu.make_async_copy(
-                    part.at[pl.ds(first + c * chunk, chunk)],
-                    held.at[pl.ds(a * half + c * chunk, chunk)],
-                    sems.at[a * steps + c],
-                ).start()
+
+        @pl.when(counts[a // 2] > 0)
+        def _():
+            pltpu.make_async_copy(
+                part.at[pl.ds(first, half)], held.at[pl.ds(a * half, half)], sems.at[a]
+            ).start()
 
     used = acc.at[pl.ds(1, rows)]
     state_copies = [
@@ -106,23 +102,25 @@
     if has_acc:
         acc_copy.wait()
 
-    def part_body(a, carry):
-        def chunk_body(c, inner):
-            base = a * half + c * chunk
-            pltpu.make_async_copy(
-                parts[0].at[pl.ds(0, chunk)], held.at[pl.ds(base, chunk)], sems.at[a * steps + c]
-            ).wait()
-            for j in range(chunk):
+    def group_body(g, carry):
+        base = g * group
+
+        @pl.when(counts[g] > 0)
+        def _():
+            for i in range(2):
+                pltpu.make_async_copy(
+                    parts[-1], held.at[pl.ds(base + i * half, half)], sems.at[2 * g + i]
+                ).wait()
+            for j in range(group):
                 code = codes[base + j]
                 picked = ext[code & (2**bits - 1)]
                 acc[code >> bits] += jnp.dot(
                     picked, held[base + j], preferred_element_type=jnp.float32
                 )
-            return inner
-
-        return lax.fori_loop(0, lax.div(counts[a] + chunk - 1, chunk), chunk_body, carry)
-
-    lax.fori_loop(0, len(halves), part_body, 0)
+
+        return carry
+
+    lax.fori_loop(0, len(halves) // 2, group_body, 0)
 
     if not last:
         results = [used]
@@ -152,7 +150,6 @@
 
 def sweep(parts, counts, codes, coef, fields, acc_in=None, state=None, final=False):
     half, width = min(part.shape[0] for part in parts), parts[0].shape[1]
-    chunk = min(CHUNK, half)
     held = sum(part.shape[0] for part in parts)
     rows, columns, _ = fields[1].shape
     last = state is not None
@@ -165,7 +162,7 @@
         outs = (jax.ShapeDtypeStruct(wide.shape, jnp.bfloat16), wide, wide, wide)
     extra = list(fields) + list(state or ()) + ([acc_in] if acc_in is not None else [])
     return pl.pallas_call(
-        functools.partial(sweep_kernel, len(parts), half, chunk, acc_in is not None, last, final),
+        functools.partial(sweep_kernel, len(parts), half, acc_in is not None, last, final),
         out_shape=outs,
         in_specs=[pl.BlockSpec(memory_space=pltpu.SMEM)] * 3
         + [pl.BlockSpec(memory_space=pltpu.HBM)] * (len(parts) + len(extra)),
@@ -176,7 +173,7 @@
             pltpu.VMEM((held, width, width), jnp.bfloat16),
             pltpu.VMEM((3, rows, columns, width), jnp.float32),
             pltpu.VMEM((rows, columns, width), jnp.bfloat16),
-            pltpu.SemaphoreType.DMA((held // chunk,)),
+            pltpu.SemaphoreType.DMA((held // half,)),
             pltpu.SemaphoreType.DMA((3,)),
             pltpu.SemaphoreType.DMA((4,)),
             pltpu.SemaphoreType.DMA((4,)),
@@ -258,7 +255,7 @@
     far_codes = lax.ppermute(got_codes, "rhs", ring(across, 2))
     all_codes = jnp.stack([got_codes, up, down, far_codes], axis=1)
     all_codes = all_codes.reshape(2, 4, 2, half)
-    all_counts = half * jnp.any(all_codes > 0, axis=3).astype(jnp.int32).reshape(2, 8)
+    all_counts = jnp.any(all_codes > 0, axis=(2, 3)).astype(jnp.int32)
     all_codes = all_codes.reshape(2, 4 * peers)
 
     low = low_bound[0]
@@ -275,7 +272,9 @@
     tables = (
         all_counts[0],
         all_counts[1],
-        all_counts.reshape(16),
+        all_counts.reshape(8),
+        all_counts[1, 3:],
+        all_codes[1, 3 * peers :],
         all_codes[0],
         all_codes[1],
         all_codes.reshape(8 * peers),
@@ -283,38 +282,40 @@
     )
 
     got1, *tables = lax.optimization_barrier((got1, *tables))
-    counts0, counts1, counts, codes0, codes1, codes, *coefs = tables
+    counts0, counts1, counts, counts2, codes2, codes0, codes1, codes, *coefs = tables
 
     residual = rhs_in
     direction = residual / theta
     adjoint = direction
     fields = neighbours(direction.astype(jnp.bfloat16))
 
-    def first_product(parts):
-        (acc,) = sweep(parts, counts0, codes0, coefs[0], fields)
-        return acc
-
-    def with_second(parts, got):
-        first, second = got[:half], got[half:]
+    def with_second(parts, first, second):
         up_first = lax.ppermute(first, "rhs", ring(across, 1))
         down_second = lax.ppermute(second, "rhs", ring(across, -1))
         up_second = lax.ppermute(second, "rhs", ring(across, 1))
         down_first = lax.ppermute(first, "rhs", ring(across, -1))
-        acc = first_product(parts)
+        near1 = [first, second, up_first, up_second, down_first, down_second]
         far1 = far(up_first, down_second)
-        return acc, [up_first, up_second, down_first, down_second, *far1]
-
-    def without_second(parts, got):
-        return first_product(parts), [jnp.zeros(got[:half].shape, got.dtype)] * 6
+        (acc,) = sweep(parts, counts0, codes0, coefs[0], fields)
+        (acc,) = sweep(near1, counts1, codes1, coefs[0], fields, acc)
+        return acc, near1[2:], list(far1)
+
+    def without_second(parts, first, second):
+        (acc,) = sweep(parts, counts0, codes0, coefs[0], fields)
+        blank = jnp.zeros(first.shape, first.dtype)
+        return acc, [blank] * 4, [blank] * 2
 
     parts0 = [got0, *near0, *far0]
-    acc, others1 = lax.cond(jnp.sum(counts1) > 0, with_second, without_second, parts0, got1)
-    parts1 = [got1, *others1]
+    local1 = [got1[:half], got1[half:]]
+    acc, others1, far1 = lax.cond(
+        jnp.sum(counts1) > 0, with_second, without_second, parts0, *local1
+    )
+    parts1 = [*local1, *others1, *far1]
     for number in range(ITERS):
         state = (adjoint, residual, direction)
         final = number + 1 == ITERS
         if number == 0:
-            out = sweep(parts1, counts1, codes1, coefs[0], fields, acc, state)
+            out = sweep(far1, counts2, codes2, coefs[0], fields, acc, state)
         else:
             out = sweep(
                 parts0 + parts1, counts, codes, coefs[number], fields, None, state, final

time: 311 us -> 305 us (0.981)
  waiting for transfers between devices: 183 us -> 178 us
    ppermute x1, waiting for transfers between devices: 0.01 us -> 21.8 us  [with_second(): up_first = lax.ppermute(first, 'rhs', ring(across, 1))]
    ppermute x2, waiting for transfers between devices: 21.3 us -> 0.01 us  [far(): lax.ppermute(below, 'rhs', ring(count, -1))]
    ppermute x1, waiting for transfers between devices: 20.3 us -> 0.01 us  [with_second(): down_second = lax.ppermute(second, 'rhs', ring(across, -1))]
    ppermute x2, waiting for transfers between devices: 1.22 us -> 18.1 us  [far(): lax.ppermute(above, 'rhs', ring(count, 1))]
    ppermute x1, waiting for transfers between devices: 16.9 us -> 1.22 us  [with_second(): up_second = lax.ppermute(second, 'rhs', ring(across, 1))]
    ppermute x1, waiting for transfers between devices: 0.01 us -> 13.2 us  [with_second(): down_first = lax.ppermute(first, 'rhs', ring(across, -1))]
    pallas_call x5 -> x6, Pallas kernels: 44.6 us -> 41.5 us  [sweep(): pl.pallas_call(functools.partial(sweep_kernel, len(parts), half, acc_in i...]
  transfers between devices with their start and end apart: 23 -> 23, of which waited for: 11 -> 10; matrix products, arithmetic and copies ran while one was open for 3% -> 5% of each run, Pallas kernels for 2% -> 3%
where the time goes in v2:
time: 305 us
  waiting for transfers between devices  178 us (58%)
  Pallas kernels  45.6 us (15%)
  starting transfers between devices  44.2 us (14%)
  blocking collectives  15.2 us (5%)
  local copies, waits for them, and re-layouts  13.2 us (4%)
  other arithmetic  4.61 us (2%)
  between operations  3.38 us (1%)
    all_to_all x1, waiting for transfers between devices, local_program(): lax.all_to_all(sent0, 'rows', split_axis=0, concat_axis=0, tiled=True)  49.8 us
    ppermute x1, waiting for transfers between devices, near(): lax.ppermute(packed, 'rhs', ring(count, -1))  42 us
    pallas_call x6, Pallas kernels, sweep(): pl.pallas_call(functools.partial(sweep_kernel, len(parts), half, acc_in i...  41.5 us
    ppermute x1, waiting for transfers between devices, with_second(): up_first = lax.ppermute(first, 'rhs', ring(across, 1))  21.8 us
    ppermute x1, waiting for transfers between devices, local_program(): far_codes = lax.ppermute(got_codes, 'rhs', ring(across, 2))  18.5 us
    ppermute x2, waiting for transfers between devices, far(): lax.ppermute(above, 'rhs', ring(count, 1))  18.1 us
    all_to_all x1, blocking collectives, local_program(): lax.all_to_all(send_codes.reshape(peers, 2), 'rows', split_axis=0, concat...  15.2 us
    ppermute x4, waiting for transfers between devices, neighbours(): lax.ppermute(rounded, 'rows', ring(count, -1))  13.7 us
  transfers between devices with their start and end apart: 23, of which 10 were waited for; matrix products, arithmetic and copies ran while one was open for 5% of the time, Pallas kernels for 3%

profile of v2, /device:TPU:33, one launch (start us, length us, event | category | flops | bytes accessed | tf_op | source)
XLA Modules:
  0.0 304.7 jit_solution(12216085973820738776)
XLA Ops:
  0.6 1.4 convert_reduce_fusion.place
  2.1 4.1 %form_blocks.1 = (bf16[64,128,128]{2,1,0:T(8,128)(2,1)}, bf16[64,128,128]{2,1,0:T(8,128)(2,1)}) custom-call(s32[32]{0:T(128)} %bitcast.33, s32[32]{0:T(128)} %convert_reduce_fusion.place, bf16[32,128,128]{2,1,0:T(8,128)(2,1)} %left.1, bf16[32,128,128]{2,1,0:T(8,128)(2,1)} %right.1, f32[32,128]{1,0:T(8,128)} %diag.1), custom_call_target="tpu_custom_call" | custom-call | tf_op jit(solution)/shard_map/form_blocks/pallas_call | solution.py:39
  6.2 12.2 %all-to-all-start = ((bf16[64,128,128]{2,1,0:T(8,128)(2,1)}), bf16[64,128,128]{2,1,0:T(8,128)(2,1)S(1)}, u32[]{:S(2)}, u32[]{:S(2)}) async-start(bf16[64,128,128]{2,1,0:T(8,128)(2,1)} %get-tuple-element.118), calls=%async_computation | async-start | bytes 4194304 | tf_op jit(solution)/shard_map/all_to_all | solution.py:242
  18.6 49.8 %all-to-all-done.refs_3_ = bf16[64,128,128]{2,1,0:T(8,128)(2,1)S(1)} async-done(((bf16[64,128,128]{2,1,0:T(8,128)(2,1)}), bf16[64,128,128]{2,1,0:T(8,128)(2,1)S(1)}, u32[]{:S(2)}, u32[]{:S(2)}) %all-to-all-start) | async-done | bytes 2097184 | tf_op jit(solution)/shard_map/all_to_all | solution.py:242
  68.5 15.2 %all_to_all.22 = s32[64,1,2]{2,1,0:T(1,128)S(1)} all-to-all(s32[64,1,2]{2,1,0:T(1,128)S(1)} %bitcast.23), channel_id=1, replica_groups=mesh['rows'=64,'rhs'=4] {'rows'}, dimensions={0} | all-to-all | bytes 1024 | tf_op jit(solution)/shard_map/all_to_all | solution.py:247
  83.8 6.7 %all-to-all-start.2 = ((bf16[64,128,128]{2,1,0:T(8,128)(2,1)}), bf16[64,128,128]{2,1,0:T(8,128)(2,1)}, u32[]{:S(2)}, u32[]{:S(2)}) async-start(bf16[64,128,128]{2,1,0:T(8,128)(2,1)} %get-tuple-element.120), calls=%async_computation.2 | async-start | bytes 4194304 | tf_op jit(solution)/shard_map/all_to_all | solution.py:251
  90.6 2.6 collective-permute-start.10
  95.8 42.0 %collective-permute-done.10.refs_5_ = bf16[64,128,128]{2,1,0:T(8,128)(2,1)} collective-permute-done((bf16[64,128,128]{2,1,0:T(8,128)(2,1)S(1)}, bf16[64,128,128]{2,1,0:T(8,128)(2,1)}, u32[]{:S(2)}, u32[]{:S(2)}) %collective-permute-start.10) | collective-permute-done | bytes 2097184 | tf_op jit(solution)/shard_map/ppermute | solution.py:194
  137.7 2.3 slice.46
  140.0 3.5 %collective-permute-start.12 = (bf16[32,128,128]{2,1,0:T(8,128)(2,1)}, bf16[32,128,128]{2,1,0:T(8,128)(2,1)}, u32[]{:S(2)}, u32[]{:S(2)}) collective-permute-start(bf16[32,128,128]{2,1,0:T(8,128)(2,1)} %slice.46), channel_id=1, source_target_pairs={{0,3},{1,0},{2,1},{3,2},{4,7},{5,4},{6,5},{7,6},{8,11},{9,8},{10,9... | collective-permute-start | bytes 3145736 | tf_op jit(solution)/shard_map/ppermute | solution.py:202
  143.6 2.3 slice.45
  147.8 1.5 collective-permute-start.7
  150.6 18.5 %collective-permute-done.8 = s32[2,64]{1,0:T(2,128)S(1)} collective-permute-done((s32[2,64]{1,0:T(2,128)S(1)}, s32[2,64]{1,0:T(2,128)S(1)}, u32[]{:S(2)}, u32[]{:S(2)}) %collective-permute-start.8) | collective-permute-done | bytes 544 | tf_op jit(solution)/shard_map/ppermute | solution.py:255
  169.0 2.4 collective-permute-start.14
  177.3 2.7 fusion.2
  180.0 71.1 %conditional.1 = (f32[16,64,128]{2,1,0:T(8,128)S(1)}, bf16[32,128,128]{2,1,0:T(8,128)(2,1)}, bf16[32,128,128]{2,1,0:T(8,128)(2,1)}, bf16[32,128,128]{2,1,0:T(8,1...) conditional(s32[]{:T(128)} %convert_element_type.22, ...), branch_computations={%region_4.5_spmd, %region_5.6_spmd} | conditional | bytes 25166120 | solution.py:310
  180.3 2.7 collective-permute-start.3
  183.0 1.4 collective-permute-start.1
  184.4 21.8 %collective-permute-done.refs_5_ = bf16[32,128,128]{2,1,0:T(8,128)(2,1)} collective-permute-done((bf16[32,128,128]{2,1,0:T(8,128)(2,1)}, bf16[32,128,128]{2,1,0:T(8,128)(2,1)}, u32[]{:S(2)}, u32[]{:S(2)}) %collective-permute-start) | collective-permute-done | bytes 1048608 | tf_op jit(solution)/shard_map/cond/branch_1_fun/ppermute | solution.py:293
  206.2 2.7 collective-permute-start.5
  208.9 5.4 %sweep.8.refs_12_ = f32[16,64,128]{2,1,0:T(8,128)} custom-call(s32[4]{0:T(128)S(1)} %get-tuple-element.71.refs_0_, s32[256]{0:T(256)S(1)} %get-tuple-element.72.refs_1_, f32[2]{0:T(128)S(1)} %get-tuple-element.65.refs_2_, bf16[64,128,128]{2,1,0:T(8,128)(2,1)S(1)} %get-tuple-element.73.refs_3_, bf16[64,128,128]{2,1,0:T(8,128)(2,1)} %get-tuple-element.74.refs_4_, ...), custom_call_target="tpu_custom_call" | custom-call | tf_op jit(solution)/shard_map/cond/branch_1_fun/sweep/pallas_call | solution.py:164
  214.3 13.2 %collective-permute-done.2.refs_7_ = bf16[32,128,128]{2,1,0:T(8,128)(2,1)} collective-permute-done((bf16[32,128,128]{2,1,0:T(8,128)(2,1)}, bf16[32,128,128]{2,1,0:T(8,128)(2,1)}, u32[]{:S(2)}, u32[]{:S(2)}) %collective-permute-start.2) | collective-permute-done | bytes 1048608 | tf_op jit(solution)/shard_map/cond/branch_1_fun/ppermute | solution.py:296
  228.7 4.4 %sweep.9 = f32[16,64,128]{2,1,0:T(8,128)S(1)} custom-call(s32[4]{0:T(128)S(1)} %get-tuple-element.63.refs_0_, s32[256]{0:T(256)S(1)} %get-tuple-element.64.refs_1_, f32[2]{0:T(128)S(1)} %get-tuple-element.65.refs_2_, bf16[32,128,128]{2,1,0:T(8,128)(2,1)} %get-tuple-element.66.refs_3_, bf16[32,128,128]{2,1,0:T(8,128)(2,1)S(1)} %get-tuple-element.67.refs_4_, ...), custom_call_target="tpu_custom_call" | custom-call | tf_op jit(solution)/shard_map/cond/branch_1_fun/sweep/pallas_call | solution.py:164
  233.1 18.1 %collective-permute-done.4 = bf16[32,128,128]{2,1,0:T(8,128)(2,1)} collective-permute-done((bf16[32,128,128]{2,1,0:T(8,128)(2,1)}, bf16[32,128,128]{2,1,0:T(8,128)(2,1)}, u32[]{:S(2)}, u32[]{:S(2)}) %collective-permute-start.4) | collective-permute-done | bytes 1048608 | tf_op jit(solution)/shard_map/cond/branch_1_fun/ppermute | solution.py:201
  251.2 5.1 %sweep.10 = (bf16[16,64,128]{2,1,0:T(8,128)(2,1)}, f32[16,64,128]{2,1,0:T(8,128)}, f32[16,64,128]{2,1,0:T(8,128)}, f32[16,64,128]{2,1,0:T(8,128)}) custom-call(s32[1]{0:T(128)} %bitcast.4.refs_0_, s32[64]{0:T(128)} %slice_bitcast_fusion.refs_1_, f32[2]{0:T(128)S(1)} %get-tuple-element.129.refs_2_, bf16[32,128,128]{2,1,0:T(8,128)(2,1)} %get-tuple-element.135.refs_3_.refs_14_, ...), custom_call_target="tpu_custom_call" | custom-call | tf_op jit(solution)/shard_map/sweep/pallas_call | solution.py:164
  256.3 1.3 collective-permute-start.16
  258.1 4.6 %collective-permute-done.16.refs_18_ = bf16[16,64,128]{2,1,0:T(8,128)(2,1)S(1)} collective-permute-done((bf16[16,64,128]{2,1,0:T(8,128)(2,1)}, bf16[16,64,128]{2,1,0:T(8,128)(2,1)S(1)}, u32[]{:S(2)}, u32[]{:S(2)}) %collective-permute-start.16) | collective-permute-done | bytes 262176 | tf_op jit(solution)/shard_map/ppermute | solution.py:211
  263.4 9.0 %sweep.11 = (bf16[16,64,128]{2,1,0:T(8,128)(2,1)}, f32[16,64,128]{2,1,0:T(8,128)}, f32[16,64,128]{2,1,0:T(8,128)}, f32[16,64,128]{2,1,0:T(8,128)}) custom-call(s32[8]{0:T(128)} %reshape.41.refs_0_, s32[512]{0:T(512)} %reshape_reshape_reshape.3.refs_1_, f32[2]{0:T(128)} %get-tuple-element.138.refs_2_, bf16[64,128,128]{2,1,0:T(8,128)(2,1)S(1)} %all-to-all-done.refs_3_, ...), custom_call_target="tpu_custom_call" | custom-call | tf_op jit(solution)/shard_map/sweep/pallas_call | solution.py:164
  274.3 4.6 %collective-permute-done.18.refs_18_ = bf16[16,64,128]{2,1,0:T(8,128)(2,1)S(1)} collective-permute-done((bf16[16,64,128]{2,1,0:T(8,128)(2,1)}, bf16[16,64,128]{2,1,0:T(8,128)(2,1)S(1)}, u32[]{:S(2)}, u32[]{:S(2)}) %collective-permute-start.18) | collective-permute-done | bytes 262176 | tf_op jit(solution)/shard_map/ppermute | solution.py:211
  279.6 9.0 %sweep.12 = (bf16[16,64,128]{2,1,0:T(8,128)(2,1)}, f32[16,64,128]{2,1,0:T(8,128)}, f32[16,64,128]{2,1,0:T(8,128)}, f32[16,64,128]{2,1,0:T(8,128)}) custom-call(s32[8]{0:T(128)} %reshape.41.refs_0_, s32[512]{0:T(512)} %reshape_reshape_reshape.3.refs_1_, f32[2]{0:T(128)} %get-tuple-element.137.refs_2_, bf16[64,128,128]{2,1,0:T(8,128)(2,1)S(1)} %all-to-all-done.refs_3_, ...), custom_call_target="tpu_custom_call" | custom-call | tf_op jit(solution)/shard_map/sweep/pallas_call | solution.py:164
  290.4 4.6 %collective-permute-done.20.refs_18_ = bf16[16,64,128]{2,1,0:T(8,128)(2,1)S(1)} collective-permute-done((bf16[16,64,128]{2,1,0:T(8,128)(2,1)}, bf16[16,64,128]{2,1,0:T(8,128)(2,1)S(1)}, u32[]{:S(2)}, u32[]{:S(2)}) %collective-permute-start.20) | collective-permute-done | bytes 262176 | tf_op jit(solution)/shard_map/ppermute | solution.py:211
  295.8 8.7 %sweep.13 = (f32[16,64,128]{2,1,0:T(8,128)}, f32[16,64,128]{2,1,0:T(8,128)}) custom-call(s32[8]{0:T(128)} %reshape.41.refs_0_, s32[512]{0:T(512)} %reshape_reshape_reshape.3.refs_1_, f32[2]{0:T(128)} %get-tuple-element.124.refs_2_, bf16[64,128,128]{2,1,0:T(8,128)(2,1)S(1)} %all-to-all-done.refs_3_, bf16[64,128,128]{2,1,0:T(8,128)(2,1)} %collective-permute-done.9.refs_4_, ...), custom_call_target="tpu_custom_call" | custom-call | tf_op jit(solution)/shard_map/sweep/pallas_call | solution.py:164
  (77 shorter events, 17.5 us)
Async XLA Ops:
  6.2 12.3 %copy-start.7 = (s32[32,1]{0,1:T(1,128)S(1)}, s32[32,1]{0,1:T(1,128)}, u32[]{:S(2)}) copy-start(s32[32,1]{0,1:T(1,128)} %param.15) | copy-start | bytes 388
  6.2 12.3 %copy-start.8 = (s32[32]{0:T(128)S(1)}, s32[32]{0:T(128)}, u32[]{:S(2)}) copy-start(s32[32]{0:T(128)} %convert_reduce_fusion.place) | copy-start | bytes 388
  6.2 12.3 %copy-start.9 = (s32[32]{0:T(128)S(1)}, s32[32]{0:T(128)}, u32[]{:S(2)}) copy-start(s32[32]{0:T(128)} %param.18) | copy-start | bytes 388
  6.2 12.3 %copy-start.10 = (s32[32]{0:T(128)S(1)}, s32[32]{0:T(128)}, u32[]{:S(2)}) copy-start(s32[32]{0:T(128)} %param.17) | copy-start | bytes 388
  6.2 12.3 %copy-start.11 = (s32[32]{0:T(128)S(1)}, s32[32]{0:T(128)}, u32[]{:S(2)}) copy-start(s32[32]{0:T(128)} %param.16) | copy-start | bytes 388
  6.2 62.2 %all-to-all-start = ((bf16[64,128,128]{2,1,0:T(8,128)(2,1)}), bf16[64,128,128]{2,1,0:T(8,128)(2,1)S(1)}, u32[]{:S(2)}, u32[]{:S(2)}) async-start(bf16[64,128,128]{2,1,0:T(8,128)(2,1)} %get-tuple-element.118), calls=%async_computation | async-start | bytes 4194304 | tf_op jit(solution)/shard_map/all_to_all | solution.py:242
  83.8 11.0 %copy-start = (f32[16,64,128]{2,1,0:T(8,128)S(1)}, f32[16,64,128]{2,1,0:T(8,128)}, u32[]{:S(2)}) copy-start(f32[16,64,128]{2,1,0:T(8,128)} %refs_9_.1) | copy-start | bytes 1572868
  83.8 92.2 %all-to-all-start.2 = ((bf16[64,128,128]{2,1,0:T(8,128)(2,1)}), bf16[64,128,128]{2,1,0:T(8,128)(2,1)}, u32[]{:S(2)}, u32[]{:S(2)}) async-start(bf16[64,128,128]{2,1,0:T(8,128)(2,1)} %get-tuple-element.120), calls=%async_computation.2 | async-start | bytes 4194304 | tf_op jit(solution)/shard_map/all_to_all | solution.py:251
  90.6 47.2 %collective-permute-start.10 = (bf16[64,128,128]{2,1,0:T(8,128)(2,1)S(1)}, bf16[64,128,128]{2,1,0:T(8,128)(2,1)}, u32[]{:S(2)}, u32[]{:S(2)}) collective-permute-start(bf16[64,128,128]{2,1,0:T(8,128)(2,1)S(1)} %all-to-all-done.refs_3_), channel_id=1, source_target_pairs={{0,3},{1,0},{2,1},{3,2},{4,7},{5,4},{6,5},{7,6},{8,11},{9,8},{10,9... | collective-permute-start | bytes 6291464 | tf_op jit(solution)/shard_map/ppermute | solution.py:194
  93.1 50.4 %collective-permute-start.9 = (bf16[64,128,128]{2,1,0:T(8,128)(2,1)S(1)}, bf16[64,128,128]{2,1,0:T(8,128)(2,1)}, u32[]{:S(2)}, u32[]{:S(2)}) collective-permute-start(bf16[64,128,128]{2,1,0:T(8,128)(2,1)S(1)} %all-to-all-done.refs_3_), channel_id=1, source_target_pairs={{0,1},{1,2},{2,3},{3,0},{4,5},{5,6},{6,7},{7,4},{8,9},{9,10},{10,1... | collective-permute-start | bytes 6291464 | tf_op jit(solution)/shard_map/ppermute | solution.py:193
  140.0 40.0 %collective-permute-start.12 = (bf16[32,128,128]{2,1,0:T(8,128)(2,1)}, bf16[32,128,128]{2,1,0:T(8,128)(2,1)}, u32[]{:S(2)}, u32[]{:S(2)}) collective-permute-start(bf16[32,128,128]{2,1,0:T(8,128)(2,1)} %slice.46), channel_id=1, source_target_pairs={{0,3},{1,0},{2,1},{3,2},{4,7},{5,4},{6,5},{7,6},{8,11},{9,8},{10,9... | collective-permute-start | bytes 3145736 | tf_op jit(solution)/shard_map/ppermute | solution.py:202
  145.9 34.1 %collective-permute-start.11 = (bf16[32,128,128]{2,1,0:T(8,128)(2,1)}, bf16[32,128,128]{2,1,0:T(8,128)(2,1)}, u32[]{:S(2)}, u32[]{:S(2)}) collective-permute-start(bf16[32,128,128]{2,1,0:T(8,128)(2,1)} %slice.45), channel_id=1, source_target_pairs={{0,1},{1,2},{2,3},{3,0},{4,5},{5,6},{6,7},{7,4},{8,9},{9,10},{10,1... | collective-permute-start | bytes 3145736 | tf_op jit(solution)/shard_map/ppermute | solution.py:201
  146.6 22.5 %collective-permute-start.8 = (s32[2,64]{1,0:T(2,128)S(1)}, s32[2,64]{1,0:T(2,128)S(1)}, u32[]{:S(2)}, u32[]{:S(2)}) collective-permute-start(s32[2,64]{1,0:T(2,128)S(1)} %bitcast.24), channel_id=1, source_target_pairs={{0,2},{1,3},{2,0},{3,1},{4,6},{5,7},{6,4},{7,5},{8,10},{9,11},{10,... | collective-permute-start | bytes 1544 | tf_op jit(solution)/shard_map/ppermute | solution.py:255
  147.8 23.8 %collective-permute-start.7 = (s32[2,64]{1,0:T(2,128)S(1)}, s32[2,64]{1,0:T(2,128)S(1)}, u32[]{:S(2)}, u32[]{:S(2)}) collective-permute-start(s32[2,64]{1,0:T(2,128)S(1)} %bitcast.25), channel_id=1, source_target_pairs={{0,3},{1,0},{2,1},{3,2},{4,7},{5,4},{6,5},{7,6},{8,11},{9,8},{10,9... | collective-permute-start | bytes 1544 | tf_op jit(solution)/shard_map/ppermute | solution.py:254
  149.2 23.5 %collective-permute-start.6 = (s32[2,64]{1,0:T(2,128)S(1)}, s32[2,64]{1,0:T(2,128)S(1)}, u32[]{:S(2)}, u32[]{:S(2)}) collective-permute-start(s32[2,64]{1,0:T(2,128)S(1)} %bitcast.26), channel_id=1, source_target_pairs={{0,1},{1,2},{2,3},{3,0},{4,5},{5,6},{6,7},{7,4},{8,9},{9,10},{10,1... | collective-permute-start | bytes 1544 | tf_op jit(solution)/shard_map/ppermute | solution.py:253
  169.0 11.0 %collective-permute-start.14 = (bf16[16,64,128]{2,1,0:T(8,128)(2,1)S(1)}, bf16[16,64,128]{2,1,0:T(8,128)(2,1)}, u32[]{:S(2)}, u32[]{:S(2)}) collective-permute-start(bf16[16,64,128]{2,1,0:T(8,128)(2,1)S(1)} %get-tuple-element.158.refs_6_), channel_id=1, source_target_pairs={{0,252},{4,0},{8,4},{12,8},{16,12},{20,16},{24,20},{28,24},{32,28}... | collective-permute-start | bytes 786440 | tf_op jit(solution)/shard_map/ppermute | solution.py:211
  171.5 8.5 %collective-permute-start.13 = (bf16[16,64,128]{2,1,0:T(8,128)(2,1)S(1)}, bf16[16,64,128]{2,1,0:T(8,128)(2,1)}, u32[]{:S(2)}, u32[]{:S(2)}) collective-permute-start(bf16[16,64,128]{2,1,0:T(8,128)(2,1)S(1)} %get-tuple-element.158.refs_6_), channel_id=1, source_target_pairs={{0,4},{4,8},{8,12},{12,16},{16,20},{20,24},{24,28},{28,32},{32,36}... | collective-permute-start | bytes 786440 | tf_op jit(solution)/shard_map/ppermute | solution.py:209
  180.2 26.0 %collective-permute-start = (bf16[32,128,128]{2,1,0:T(8,128)(2,1)}, bf16[32,128,128]{2,1,0:T(8,128)(2,1)}, u32[]{:S(2)}, u32[]{:S(2)}) collective-permute-start(bf16[32,128,128]{2,1,0:T(8,128)(2,1)} %get-tuple-element.66.refs_3_), channel_id=1, source_target_pairs={{0,1},{1,2},{2,3},{3,0},{4,5},{5,6},{6,7},{7,4},{8,9},{9,10},{10,1... | collective-permute-start | bytes 3145736 | tf_op jit(solution)/shard_map/cond/branch_1_fun/ppermute | solution.py:293
  180.3 25.9 %collective-permute-start.3 = (bf16[32,128,128]{2,1,0:T(8,128)(2,1)S(1)}, bf16[32,128,128]{2,1,0:T(8,128)(2,1)}, u32[]{:S(2)}, u32[]{:S(2)}) collective-permute-start(bf16[32,128,128]{2,1,0:T(8,128)(2,1)S(1)} %get-tuple-element.67.refs_4_), channel_id=1, source_target_pairs={{0,3},{1,0},{2,1},{3,2},{4,7},{5,4},{6,5},{7,6},{8,11},{9,8},{10,9... | collective-permute-start | bytes 3145736 | tf_op jit(solution)/shard_map/cond/branch_1_fun/ppermute | solution.py:294
  183.0 44.5 %collective-permute-start.2 = (bf16[32,128,128]{2,1,0:T(8,128)(2,1)}, bf16[32,128,128]{2,1,0:T(8,128)(2,1)}, u32[]{:S(2)}, u32[]{:S(2)}) collective-permute-start(bf16[32,128,128]{2,1,0:T(8,128)(2,1)} %get-tuple-element.66.refs_3_), channel_id=1, source_target_pairs={{0,3},{1,0},{2,1},{3,2},{4,7},{5,4},{6,5},{7,6},{8,11},{9,8},{10,9... | collective-permute-start | bytes 3145736 | tf_op jit(solution)/shard_map/cond/branch_1_fun/ppermute | solution.py:296
  183.0 45.7 %collective-permute-start.1 = (bf16[32,128,128]{2,1,0:T(8,128)(2,1)S(1)}, bf16[32,128,128]{2,1,0:T(8,128)(2,1)}, u32[]{:S(2)}, u32[]{:S(2)}) collective-permute-start(bf16[32,128,128]{2,1,0:T(8,128)(2,1)S(1)} %get-tuple-element.67.refs_4_), channel_id=1, source_target_pairs={{0,1},{1,2},{2,3},{3,0},{4,5},{5,6},{6,7},{7,4},{8,9},{9,10},{10,1... | collective-permute-start | bytes 3145736 | tf_op jit(solution)/shard_map/cond/branch_1_fun/ppermute | solution.py:295
  206.2 44.9 %collective-permute-start.4 = (bf16[32,128,128]{2,1,0:T(8,128)(2,1)}, bf16[32,128,128]{2,1,0:T(8,128)(2,1)}, u32[]{:S(2)}, u32[]{:S(2)}) collective-permute-start(bf16[32,128,128]{2,1,0:T(8,128)(2,1)} %collective-permute-done.refs_5_), channel_id=1, source_target_pairs={{0,1},{1,2},{2,3},{3,0},{4,5},{5,6},{6,7},{7,4},{8,9},{9,10},{10,1... | collective-permute-start | bytes 3145736 | tf_op jit(solution)/shard_map/cond/branch_1_fun/ppermute | solution.py:201
  206.2 44.9 %collective-permute-start.5 = (bf16[32,128,128]{2,1,0:T(8,128)(2,1)}, bf16[32,128,128]{2,1,0:T(8,128)(2,1)}, u32[]{:S(2)}, u32[]{:S(2)}) collective-permute-start(bf16[32,128,128]{2,1,0:T(8,128)(2,1)} %collective-permute-done.3.refs_8_), channel_id=1, source_target_pairs={{0,3},{1,0},{2,1},{3,2},{4,7},{5,4},{6,5},{7,6},{8,11},{9,8},{10,9... | collective-permute-start | bytes 3145736 | tf_op jit(solution)/shard_map/cond/branch_1_fun/ppermute | solution.py:202
  256.3 6.4 %collective-permute-start.16 = (bf16[16,64,128]{2,1,0:T(8,128)(2,1)}, bf16[16,64,128]{2,1,0:T(8,128)(2,1)S(1)}, u32[]{:S(2)}, u32[]{:S(2)}) collective-permute-start(bf16[16,64,128]{2,1,0:T(8,128)(2,1)} %get-tuple-element.142.refs_17_), channel_id=1, source_target_pairs={{0,252},{4,0},{8,4},{12,8},{16,12},{20,16},{24,20},{28,24},{32,28}... | collective-permute-start | bytes 786440 | tf_op jit(solution)/shard_map/ppermute | solution.py:211
  257.5 5.1 %collective-permute-start.15 = (bf16[16,64,128]{2,1,0:T(8,128)(2,1)}, bf16[16,64,128]{2,1,0:T(8,128)(2,1)S(1)}, u32[]{:S(2)}, u32[]{:S(2)}) collective-permute-start(bf16[16,64,128]{2,1,0:T(8,128)(2,1)} %get-tuple-element.142.refs_17_), channel_id=1, source_target_pairs={{0,4},{4,8},{8,12},{12,16},{16,20},{20,24},{24,28},{28,32},{32,36}... | collective-permute-start | bytes 786440 | tf_op jit(solution)/shard_map/ppermute | solution.py:209
  262.7 0.8 copy-start.5
  272.5 6.4 %collective-permute-start.18 = (bf16[16,64,128]{2,1,0:T(8,128)(2,1)}, bf16[16,64,128]{2,1,0:T(8,128)(2,1)S(1)}, u32[]{:S(2)}, u32[]{:S(2)}) collective-permute-start(bf16[16,64,128]{2,1,0:T(8,128)(2,1)} %get-tuple-element.146.refs_17_), channel_id=1, source_target_pairs={{0,252},{4,0},{8,4},{12,8},{16,12},{20,16},{24,20},{28,24},{32,28}... | collective-permute-start | bytes 786440 | tf_op jit(solution)/shard_map/ppermute | solution.py:211
  273.4 5.4 %collective-permute-start.17 = (bf16[16,64,128]{2,1,0:T(8,128)(2,1)}, bf16[16,64,128]{2,1,0:T(8,128)(2,1)S(1)}, u32[]{:S(2)}, u32[]{:S(2)}) collective-permute-start(bf16[16,64,128]{2,1,0:T(8,128)(2,1)} %get-tuple-element.146.refs_17_), channel_id=1, source_target_pairs={{0,4},{4,8},{8,12},{12,16},{16,20},{20,24},{24,28},{28,32},{32,36}... | collective-permute-start | bytes 786440 | tf_op jit(solution)/shard_map/ppermute | solution.py:209
  278.8 0.8 copy-start.6
  288.6 6.4 %collective-permute-start.20 = (bf16[16,64,128]{2,1,0:T(8,128)(2,1)}, bf16[16,64,128]{2,1,0:T(8,128)(2,1)S(1)}, u32[]{:S(2)}, u32[]{:S(2)}) collective-permute-start(bf16[16,64,128]{2,1,0:T(8,128)(2,1)} %get-tuple-element.150.refs_17_), channel_id=1, source_target_pairs={{0,252},{4,0},{8,4},{12,8},{16,12},{20,16},{24,20},{28,24},{32,28}... | collective-permute-start | bytes 786440 | tf_op jit(solution)/shard_map/ppermute | solution.py:211
  289.3 5.7 %collective-permute-start.19 = (bf16[16,64,128]{2,1,0:T(8,128)(2,1)}, bf16[16,64,128]{2,1,0:T(8,128)(2,1)S(1)}, u32[]{:S(2)}, u32[]{:S(2)}) collective-permute-start(bf16[16,64,128]{2,1,0:T(8,128)(2,1)} %get-tuple-element.150.refs_17_), channel_id=1, source_target_pairs={{0,4},{4,8},{8,12},{12,16},{16,20},{20,24},{24,28},{28,32},{32,36}... | collective-permute-start | bytes 786440 | tf_op jit(solution)/shard_map/ppermute | solution.py:209
  295.0 0.8 copy-start.2
  (3 other events, 2.1 us)

commit v3 on v2

--- a/solution.py
+++ b/solution.py
@@ -61,9 +61,9 @@
     refs = refs[3:]
     parts, refs = refs[:num_parts], refs[num_parts:]
     fields, refs = refs[:3], refs[3:]
-    num_state = 3 * last + has_acc
+    num_state = (2 if final else 3 * last) + has_acc
     state, refs = refs[:num_state], refs[num_state:]
-    num_outs = (2 if final else 4) if last else 1
+    num_outs = 4 if last and not final else 1
     outs, refs = refs[:num_outs], refs[num_outs:]
     ext, acc, held, kept, rounded, sems, field_sems, state_sems, out_sems = refs
     rows = fields[1].shape[0]
@@ -87,7 +87,7 @@
     used = acc.at[pl.ds(1, rows)]
     state_copies = [
         pltpu.make_async_copy(array, kept.at[i], state_sems.at[i])
-        for i, array in enumerate(state[: 3 * last])
+        for i, array in enumerate(state[: num_state - has_acc])
     ]
     if has_acc:
         acc_copy = pltpu.make_async_copy(state[-1], used, state_sems.at[3])
@@ -127,11 +127,11 @@
     else:
         for copy in state_copies:
             copy.wait()
-        adjoint, residual, direction = (kept.at[i] for i in range(3))
+        residual, direction, adjoint = (kept.at[i] for i in range(3))
         step = direction[...]
         left = residual[...] - (step - used[...])
         residual[...] = left
-        results = [adjoint, residual]
+        results = [residual]
         if not final:
             step = coef[0] * step + coef[1] * left
             rounded[...] = step.astype(jnp.bfloat16)
@@ -157,7 +157,7 @@
     if not last:
         outs = (wide,)
     elif final:
-        outs = (wide, wide)
+        outs = (wide,)
     else:
         outs = (jax.ShapeDtypeStruct(wide.shape, jnp.bfloat16), wide, wide, wide)
     extra = list(fields) + list(state or ()) + ([acc_in] if acc_in is not None else [])
@@ -178,7 +178,7 @@
             pltpu.SemaphoreType.DMA((4,)),
             pltpu.SemaphoreType.DMA((4,)),
         ],
-        compiler_params=pltpu.CompilerParams(vmem_limit_bytes=60 * 2**20),
+        compiler_params=pltpu.CompilerParams(vmem_limit_bytes=48 * 2**20),
         name="sweep",
     )(counts, codes, coef, *parts, *extra)
 
@@ -312,8 +312,8 @@
     )
     parts1 = [*local1, *others1, *far1]
     for number in range(ITERS):
-        state = (adjoint, residual, direction)
         final = number + 1 == ITERS
+        state = (residual, direction) if final else (residual, direction, adjoint)
         if number == 0:
             out = sweep(far1, counts2, codes2, coefs[0], fields, acc, state)
         else:
@@ -321,7 +321,7 @@
                 parts0 + parts1, counts, codes, coefs[number], fields, None, state, final
             )
         if final:
-            return out
+            return adjoint, out[0]
         rounded, adjoint, residual, direction = out
         fields = neighbours(rounded)
 

time: 305 us -> 299 us (0.980)
  the two profiles are of different devices: /device:TPU:33 before, /device:TPU:38 now
where the time goes in v3:
time: 299 us; the launch traced here: 298 us
  waiting for transfers between devices  183 us (61%)
  Pallas kernels  41.5 us (14%)
  starting transfers between devices  40.8 us (14%)
  blocking collectives  15.7 us (5%)
  local copies, waits for them, and re-layouts  10.4 us (3%)
  between operations  3.46 us (1%)
    all_to_all x1, waiting for transfers between devices, local_program(): lax.all_to_all(sent0, 'rows', split_axis=0, concat_axis=0, tiled=True)  49.5 us
    ppermute x1, waiting for transfers between devices, near(): lax.ppermute(packed, 'rhs', ring(count, -1))  43.9 us
    pallas_call x6, Pallas kernels, sweep(): pl.pallas_call(functools.partial(sweep_kernel, len(parts), half, acc_in i...  37.4 us
    ppermute x1, waiting for transfers between devices, with_second(): up_first = lax.ppermute(first, 'rhs', ring(across, 1))  20.3 us
    ppermute x1, waiting for transfers between devices, with_second(): down_first = lax.ppermute(first, 'rhs', ring(across, -1))  17.9 us
    all_to_all x1, blocking collectives, local_program(): lax.all_to_all(send_codes.reshape(peers, 2), 'rows', split_axis=0, concat...  15.7 us
    ppermute x1, waiting for transfers between devices, local_program(): far_codes = lax.ppermute(got_codes, 'rhs', ring(across, 2))  14.3 us
    ppermute x2, waiting for transfers between devices, far(): lax.ppermute(above, 'rhs', ring(count, 1))  14.1 us
  transfers between devices with their start and end apart: 23, of which 15 were waited for; matrix products, arithmetic and copies ran while one was open for 3% of the time, Pallas kernels for 3%

profile of v3, /device:TPU:38, one launch (start us, length us, event | category | flops | bytes accessed | tf_op | source)
XLA Modules:
  0.0 297.9 jit_solution(13347485634440769086)
XLA Ops:
  2.1 4.1 %form_blocks.1 = (bf16[64,128,128]{2,1,0:T(8,128)(2,1)}, bf16[64,128,128]{2,1,0:T(8,128)(2,1)}) custom-call(s32[32]{0:T(128)} %bitcast.33, s32[32]{0:T(128)} %convert_reduce_fusion.place, bf16[32,128,128]{2,1,0:T(8,128)(2,1)} %left.1, bf16[32,128,128]{2,1,0:T(8,128)(2,1)} %right.1, f32[32,128]{1,0:T(8,128)} %diag.1), custom_call_target="tpu_custom_call" | custom-call | tf_op jit(solution)/shard_map/form_blocks/pallas_call | solution.py:39
  6.2 11.9 %all-to-all-start = ((bf16[64,128,128]{2,1,0:T(8,128)(2,1)}), bf16[64,128,128]{2,1,0:T(8,128)(2,1)S(1)}, u32[]{:S(2)}, u32[]{:S(2)}) async-start(bf16[64,128,128]{2,1,0:T(8,128)(2,1)} %get-tuple-element.118), calls=%async_computation | async-start | bytes 4194304 | tf_op jit(solution)/shard_map/all_to_all | solution.py:242
  18.3 49.5 %all-to-all-done.refs_3_ = bf16[64,128,128]{2,1,0:T(8,128)(2,1)S(1)} async-done(((bf16[64,128,128]{2,1,0:T(8,128)(2,1)}), bf16[64,128,128]{2,1,0:T(8,128)(2,1)S(1)}, u32[]{:S(2)}, u32[]{:S(2)}) %all-to-all-start) | async-done | bytes 2097184 | tf_op jit(solution)/shard_map/all_to_all | solution.py:242
  68.0 15.7 %all_to_all.22 = s32[64,1,2]{2,1,0:T(1,128)S(1)} all-to-all(s32[64,1,2]{2,1,0:T(1,128)S(1)} %bitcast.23), channel_id=1, replica_groups=mesh['rows'=64,'rhs'=4] {'rows'}, dimensions={0} | all-to-all | bytes 1024 | tf_op jit(solution)/shard_map/all_to_all | solution.py:247
  83.8 6.5 %all-to-all-start.2 = ((bf16[64,128,128]{2,1,0:T(8,128)(2,1)}), bf16[64,128,128]{2,1,0:T(8,128)(2,1)}, u32[]{:S(2)}, u32[]{:S(2)}) async-start(bf16[64,128,128]{2,1,0:T(8,128)(2,1)} %get-tuple-element.120), calls=%async_computation.2 | async-start | bytes 4194304 | tf_op jit(solution)/shard_map/all_to_all | solution.py:251
  91.2 2.4 collective-permute-start.9
  95.4 43.9 %collective-permute-done.10.refs_5_ = bf16[64,128,128]{2,1,0:T(8,128)(2,1)} collective-permute-done((bf16[64,128,128]{2,1,0:T(8,128)(2,1)S(1)}, bf16[64,128,128]{2,1,0:T(8,128)(2,1)}, u32[]{:S(2)}, u32[]{:S(2)}) %collective-permute-start.10) | collective-permute-done | bytes 2097184 | tf_op jit(solution)/shard_map/ppermute | solution.py:194
  139.3 2.3 slice.46
  141.6 2.3 slice.45
  144.0 3.2 %collective-permute-start.11 = (bf16[32,128,128]{2,1,0:T(8,128)(2,1)}, bf16[32,128,128]{2,1,0:T(8,128)(2,1)}, u32[]{:S(2)}, u32[]{:S(2)}) collective-permute-start(bf16[32,128,128]{2,1,0:T(8,128)(2,1)} %slice.45), channel_id=1, source_target_pairs={{0,1},{1,2},{2,3},{3,0},{4,5},{5,6},{6,7},{7,4},{8,9},{9,10},{10,1... | collective-permute-start | bytes 3145736 | tf_op jit(solution)/shard_map/ppermute | solution.py:201
  148.2 2.5 collective-permute-start.6
  150.8 14.3 %collective-permute-done.8 = s32[2,64]{1,0:T(2,128)S(1)} collective-permute-done((s32[2,64]{1,0:T(2,128)S(1)}, s32[2,64]{1,0:T(2,128)S(1)}, u32[]{:S(2)}, u32[]{:S(2)}) %collective-permute-start.8) | collective-permute-done | bytes 544 | tf_op jit(solution)/shard_map/ppermute | solution.py:255
  165.2 2.4 collective-permute-done.7
  175.2 74.9 %conditional.1 = (f32[16,64,128]{2,1,0:T(8,128)S(1)}, bf16[32,128,128]{2,1,0:T(8,128)(2,1)}, bf16[32,128,128]{2,1,0:T(8,128)(2,1)}, bf16[32,128,128]{2,1,0:T(8,1...) conditional(s32[]{:T(128)} %convert_element_type.22, ...), branch_computations={%region_4.5_spmd, %region_5.6_spmd} | conditional | bytes 25166120 | solution.py:310
  175.2 3.7 %collective-permute-start = (bf16[32,128,128]{2,1,0:T(8,128)(2,1)S(1)}, bf16[32,128,128]{2,1,0:T(8,128)(2,1)}, u32[]{:S(2)}, u32[]{:S(2)}) collective-permute-start(bf16[32,128,128]{2,1,0:T(8,128)(2,1)S(1)} %get-tuple-element.66.refs_3_), channel_id=1, source_target_pairs={{0,1},{1,2},{2,3},{3,0},{4,5},{5,6},{6,7},{7,4},{8,9},{9,10},{10,1... | collective-permute-start | bytes 3145736 | tf_op jit(solution)/shard_map/cond/branch_1_fun/ppermute | solution.py:293
  179.4 2.8 collective-permute-start.1
  182.2 20.3 %collective-permute-done.refs_5_ = bf16[32,128,128]{2,1,0:T(8,128)(2,1)} collective-permute-done((bf16[32,128,128]{2,1,0:T(8,128)(2,1)S(1)}, bf16[32,128,128]{2,1,0:T(8,128)(2,1)}, u32[]{:S(2)}, u32[]{:S(2)}) %collective-permute-start) | collective-permute-done | bytes 1048608 | tf_op jit(solution)/shard_map/cond/branch_1_fun/ppermute | solution.py:293
  202.5 3.8 %collective-permute-start.4 = (bf16[32,128,128]{2,1,0:T(8,128)(2,1)}, bf16[32,128,128]{2,1,0:T(8,128)(2,1)}, u32[]{:S(2)}, u32[]{:S(2)}) collective-permute-start(bf16[32,128,128]{2,1,0:T(8,128)(2,1)} %collective-permute-done.refs_5_), channel_id=1, source_target_pairs={{0,1},{1,2},{2,3},{3,0},{4,5},{5,6},{6,7},{7,4},{8,9},{9,10},{10,1... | collective-permute-start | bytes 3145736 | tf_op jit(solution)/shard_map/cond/branch_1_fun/ppermute | solution.py:201
  206.3 4.6 %sweep.8.refs_12_ = f32[16,64,128]{2,1,0:T(8,128)S(1)} custom-call(s32[4]{0:T(128)S(1)} %get-tuple-element.71.refs_0_, s32[256]{0:T(256)S(1)} %get-tuple-element.72.refs_1_, f32[2]{0:T(128)S(1)} %get-tuple-element.65.refs_2_, bf16[64,128,128]{2,1,0:T(8,128)(2,1)S(1)} %get-tuple-element.73.refs_3_, bf16[64,128,128]{2,1,0:T(8,128)(2,1)} %get-tuple-element.74.refs_4_, ...), custom_call_target="tpu_custom_call" | custom-call | tf_op jit(solution)/shard_map/cond/branch_1_fun/sweep/pallas_call | solution.py:164
  210.9 17.9 %collective-permute-done.2.refs_7_ = bf16[32,128,128]{2,1,0:T(8,128)(2,1)} collective-permute-done((bf16[32,128,128]{2,1,0:T(8,128)(2,1)S(1)}, bf16[32,128,128]{2,1,0:T(8,128)(2,1)}, u32[]{:S(2)}, u32[]{:S(2)}) %collective-permute-start.2) | collective-permute-done | bytes 1048608 | tf_op jit(solution)/shard_map/cond/branch_1_fun/ppermute | solution.py:296
  228.8 3.9 %sweep.9 = f32[16,64,128]{2,1,0:T(8,128)S(1)} custom-call(s32[4]{0:T(128)S(1)} %get-tuple-element.63.refs_0_, s32[256]{0:T(256)S(1)} %get-tuple-element.64.refs_1_, f32[2]{0:T(128)S(1)} %get-tuple-element.65.refs_2_, bf16[32,128,128]{2,1,0:T(8,128)(2,1)S(1)} %get-tuple-element.66.refs_3_, bf16[32,128,128]{2,1,0:T(8,128)(2,1)S(1)} %get-tuple-element.67.refs_4_, ...), custom_call_target="tpu_custom_call" | custom-call | tf_op jit(solution)/shard_map/cond/branch_1_fun/sweep/pallas_call | solution.py:164
  232.7 14.1 %collective-permute-done.4 = bf16[32,128,128]{2,1,0:T(8,128)(2,1)} collective-permute-done((bf16[32,128,128]{2,1,0:T(8,128)(2,1)}, bf16[32,128,128]{2,1,0:T(8,128)(2,1)}, u32[]{:S(2)}, u32[]{:S(2)}) %collective-permute-start.4) | collective-permute-done | bytes 1048608 | tf_op jit(solution)/shard_map/cond/branch_1_fun/ppermute | solution.py:201
  246.8 3.4 %collective-permute-done.5 = bf16[32,128,128]{2,1,0:T(8,128)(2,1)} collective-permute-done((bf16[32,128,128]{2,1,0:T(8,128)(2,1)}, bf16[32,128,128]{2,1,0:T(8,128)(2,1)}, u32[]{:S(2)}, u32[]{:S(2)}) %collective-permute-start.5) | collective-permute-done | bytes 1048608 | tf_op jit(solution)/shard_map/cond/branch_1_fun/ppermute | solution.py:202
  251.0 4.3 %sweep.10 = (bf16[16,64,128]{2,1,0:T(8,128)(2,1)S(1)}, f32[16,64,128]{2,1,0:T(8,128)S(1)}, f32[16,64,128]{2,1,0:T(8,128)S(1)}, f32[16,64,128]{2,1,0:T(8,128)S(1)}) custom-call(s32[1]{0:T(128)} %bitcast.4.refs_0_, s32[64]{0:T(128)S(1)} %slice_bitcast_fusion.refs_1_, f32[2]{0:T(128)S(1)} %get-tuple-element.129.refs_2_, ...), custom_call_target="tpu_custom_call" | custom-call | tf_op jit(solution)/shard_map/sweep/pallas_call | solution.py:164
  255.9 3.4 %collective-permute-done.16.refs_18_ = bf16[16,64,128]{2,1,0:T(8,128)(2,1)S(1)} collective-permute-done((bf16[16,64,128]{2,1,0:T(8,128)(2,1)S(1)}, bf16[16,64,128]{2,1,0:T(8,128)(2,1)S(1)}, u32[]{:S(2)}, u32[]{:S(2)}) %collective-permute-start.16) | collective-permute-done | bytes 262176 | tf_op jit(solution)/shard_map/ppermute | solution.py:211
  259.3 2.0 collective-permute-done.15.refs_16_
  261.3 7.8 %sweep.11 = (bf16[16,64,128]{2,1,0:T(8,128)(2,1)S(1)}, f32[16,64,128]{2,1,0:T(8,128)S(1)}, f32[16,64,128]{2,1,0:T(8,128)S(1)}, f32[16,64,128]{2,1,0:T(8,128)S(1)}) custom-call(s32[8]{0:T(128)S(1)} %reshape.41.refs_0_, s32[512]{0:T(512)S(1)} %reshape_reshape_reshape.3.refs_1_, f32[2]{0:T(128)S(1)} %get-tuple-element.137.refs_2_, ...), custom_call_target="tpu_custom_call" | custom-call | tf_op jit(solution)/shard_map/sweep/pallas_call | solution.py:164
  269.6 3.4 %collective-permute-done.18.refs_18_ = bf16[16,64,128]{2,1,0:T(8,128)(2,1)S(1)} collective-permute-done((bf16[16,64,128]{2,1,0:T(8,128)(2,1)S(1)}, bf16[16,64,128]{2,1,0:T(8,128)(2,1)S(1)}, u32[]{:S(2)}, u32[]{:S(2)}) %collective-permute-start.18) | collective-permute-done | bytes 262176 | tf_op jit(solution)/shard_map/ppermute | solution.py:211
  273.0 2.0 collective-permute-done.17.refs_16_
  275.0 8.5 %sweep.12 = (bf16[16,64,128]{2,1,0:T(8,128)(2,1)S(1)}, f32[16,64,128]{2,1,0:T(8,128)}, f32[16,64,128]{2,1,0:T(8,128)S(1)}, f32[16,64,128]{2,1,0:T(8,128)S(1)}) custom-call(s32[8]{0:T(128)S(1)} %reshape.41.refs_0_, s32[512]{0:T(512)S(1)} %reshape_reshape_reshape.3.refs_1_, f32[2]{0:T(128)S(1)} %get-tuple-element.124.refs_2_, ...), custom_call_target="tpu_custom_call" | custom-call | tf_op jit(solution)/shard_map/sweep/pallas_call | solution.py:164
  284.1 3.4 %collective-permute-done.20.refs_18_ = bf16[16,64,128]{2,1,0:T(8,128)(2,1)S(1)} collective-permute-done((bf16[16,64,128]{2,1,0:T(8,128)(2,1)S(1)}, bf16[16,64,128]{2,1,0:T(8,128)(2,1)S(1)}, u32[]{:S(2)}, u32[]{:S(2)}) %collective-permute-start.20) | collective-permute-done | bytes 262176 | tf_op jit(solution)/shard_map/ppermute | solution.py:211
  289.4 8.3 %sweep.13 = f32[16,64,128]{2,1,0:T(8,128)} custom-call(s32[8]{0:T(128)S(1)} %reshape.41.refs_0_, s32[512]{0:T(512)S(1)} %reshape_reshape_reshape.3.refs_1_, f32[2]{0:T(128)S(1)} %get-tuple-element.150.refs_2_, bf16[64,128,128]{2,1,0:T(8,128)(2,1)S(1)} %all-to-all-done.refs_3_, bf16[64,128,128]{2,1,0:T(8,128)(2,1)} %collective-permute-done.9.refs_4_, ...), custom_call_target="tpu_custom_call" | custom-call | tf_op jit(solution)/shard_map/sweep/pallas_call | solution.py:164
  (75 shorter events, 16.0 us)
Async XLA Ops:
  6.2 12.0 %copy-start.6 = (s32[32,1]{0,1:T(1,128)S(1)}, s32[32,1]{0,1:T(1,128)}, u32[]{:S(2)}) copy-start(s32[32,1]{0,1:T(1,128)} %param.15) | copy-start | bytes 388
  6.2 12.0 %copy-start.7 = (s32[32]{0:T(128)S(1)}, s32[32]{0:T(128)}, u32[]{:S(2)}) copy-start(s32[32]{0:T(128)} %convert_reduce_fusion.place) | copy-start | bytes 388
  6.2 12.0 %copy-start.8 = (s32[32]{0:T(128)S(1)}, s32[32]{0:T(128)}, u32[]{:S(2)}) copy-start(s32[32]{0:T(128)} %param.18) | copy-start | bytes 388
  6.2 12.0 %copy-start.9 = (s32[32]{0:T(128)S(1)}, s32[32]{0:T(128)}, u32[]{:S(2)}) copy-start(s32[32]{0:T(128)} %param.17) | copy-start | bytes 388
  6.2 12.0 %copy-start.10 = (s32[32]{0:T(128)S(1)}, s32[32]{0:T(128)}, u32[]{:S(2)}) copy-start(s32[32]{0:T(128)} %param.16) | copy-start | bytes 388
  6.2 61.6 %all-to-all-start = ((bf16[64,128,128]{2,1,0:T(8,128)(2,1)}), bf16[64,128,128]{2,1,0:T(8,128)(2,1)S(1)}, u32[]{:S(2)}, u32[]{:S(2)}) async-start(bf16[64,128,128]{2,1,0:T(8,128)(2,1)} %get-tuple-element.118), calls=%async_computation | async-start | bytes 4194304 | tf_op jit(solution)/shard_map/all_to_all | solution.py:242
  83.8 11.5 %copy-start = (f32[16,64,128]{2,1,0:T(8,128)S(1)}, f32[16,64,128]{2,1,0:T(8,128)}, u32[]{:S(2)}) copy-start(f32[16,64,128]{2,1,0:T(8,128)} %refs_8_.1) | copy-start | bytes 1572868
  83.8 87.1 %all-to-all-start.2 = ((bf16[64,128,128]{2,1,0:T(8,128)(2,1)}), bf16[64,128,128]{2,1,0:T(8,128)(2,1)}, u32[]{:S(2)}, u32[]{:S(2)}) async-start(bf16[64,128,128]{2,1,0:T(8,128)(2,1)} %get-tuple-element.120), calls=%async_computation.2 | async-start | bytes 4194304 | tf_op jit(solution)/shard_map/all_to_all | solution.py:251
  90.3 49.0 %collective-permute-start.10 = (bf16[64,128,128]{2,1,0:T(8,128)(2,1)S(1)}, bf16[64,128,128]{2,1,0:T(8,128)(2,1)}, u32[]{:S(2)}, u32[]{:S(2)}) collective-permute-start(bf16[64,128,128]{2,1,0:T(8,128)(2,1)S(1)} %all-to-all-done.refs_3_), channel_id=1, source_target_pairs={{0,3},{1,0},{2,1},{3,2},{4,7},{5,4},{6,5},{7,6},{8,11},{9,8},{10,9... | collective-permute-start | bytes 6291464 | tf_op jit(solution)/shard_map/ppermute | solution.py:194
  91.2 50.5 %collective-permute-start.9 = (bf16[64,128,128]{2,1,0:T(8,128)(2,1)S(1)}, bf16[64,128,128]{2,1,0:T(8,128)(2,1)}, u32[]{:S(2)}, u32[]{:S(2)}) collective-permute-start(bf16[64,128,128]{2,1,0:T(8,128)(2,1)S(1)} %all-to-all-done.refs_3_), channel_id=1, source_target_pairs={{0,1},{1,2},{2,3},{3,0},{4,5},{5,6},{6,7},{7,4},{8,9},{9,10},{10,1... | collective-permute-start | bytes 6291464 | tf_op jit(solution)/shard_map/ppermute | solution.py:193
  141.6 32.3 %collective-permute-start.12 = (bf16[32,128,128]{2,1,0:T(8,128)(2,1)}, bf16[32,128,128]{2,1,0:T(8,128)(2,1)}, u32[]{:S(2)}, u32[]{:S(2)}) collective-permute-start(bf16[32,128,128]{2,1,0:T(8,128)(2,1)} %slice.46), channel_id=1, source_target_pairs={{0,3},{1,0},{2,1},{3,2},{4,7},{5,4},{6,5},{7,6},{8,11},{9,8},{10,9... | collective-permute-start | bytes 3145736 | tf_op jit(solution)/shard_map/ppermute | solution.py:202
  144.0 30.0 %collective-permute-start.11 = (bf16[32,128,128]{2,1,0:T(8,128)(2,1)}, bf16[32,128,128]{2,1,0:T(8,128)(2,1)}, u32[]{:S(2)}, u32[]{:S(2)}) collective-permute-start(bf16[32,128,128]{2,1,0:T(8,128)(2,1)} %slice.45), channel_id=1, source_target_pairs={{0,1},{1,2},{2,3},{3,0},{4,5},{5,6},{6,7},{7,4},{8,9},{9,10},{10,1... | collective-permute-start | bytes 3145736 | tf_op jit(solution)/shard_map/ppermute | solution.py:201
  147.3 17.8 %collective-permute-start.8 = (s32[2,64]{1,0:T(2,128)S(1)}, s32[2,64]{1,0:T(2,128)S(1)}, u32[]{:S(2)}, u32[]{:S(2)}) collective-permute-start(s32[2,64]{1,0:T(2,128)S(1)} %bitcast.24), channel_id=1, source_target_pairs={{0,2},{1,3},{2,0},{3,1},{4,6},{5,7},{6,4},{7,5},{8,10},{9,11},{10,... | collective-permute-start | bytes 1544 | tf_op jit(solution)/shard_map/ppermute | solution.py:255
  147.3 20.2 %collective-permute-start.7 = (s32[2,64]{1,0:T(2,128)S(1)}, s32[2,64]{1,0:T(2,128)S(1)}, u32[]{:S(2)}, u32[]{:S(2)}) collective-permute-start(s32[2,64]{1,0:T(2,128)S(1)} %bitcast.25), channel_id=1, source_target_pairs={{0,3},{1,0},{2,1},{3,2},{4,7},{5,4},{6,5},{7,6},{8,11},{9,8},{10,9... | collective-permute-start | bytes 1544 | tf_op jit(solution)/shard_map/ppermute | solution.py:254
  148.2 21.0 %collective-permute-start.6 = (s32[2,64]{1,0:T(2,128)S(1)}, s32[2,64]{1,0:T(2,128)S(1)}, u32[]{:S(2)}, u32[]{:S(2)}) collective-permute-start(s32[2,64]{1,0:T(2,128)S(1)} %bitcast.26), channel_id=1, source_target_pairs={{0,1},{1,2},{2,3},{3,0},{4,5},{5,6},{6,7},{7,4},{8,9},{9,10},{10,1... | collective-permute-start | bytes 1544 | tf_op jit(solution)/shard_map/ppermute | solution.py:253
  165.1 8.8 %collective-permute-start.14 = (bf16[16,64,128]{2,1,0:T(8,128)(2,1)S(1)}, bf16[16,64,128]{2,1,0:T(8,128)(2,1)}, u32[]{:S(2)}, u32[]{:S(2)}) collective-permute-start(bf16[16,64,128]{2,1,0:T(8,128)(2,1)S(1)} %get-tuple-element.158.refs_6_), channel_id=1, source_target_pairs={{0,252},{4,0},{8,4},{12,8},{16,12},{20,16},{24,20},{28,24},{32,28}... | collective-permute-start | bytes 786440 | tf_op jit(solution)/shard_map/ppermute | solution.py:211
  167.5 6.4 %collective-permute-start.13 = (bf16[16,64,128]{2,1,0:T(8,128)(2,1)S(1)}, bf16[16,64,128]{2,1,0:T(8,128)(2,1)}, u32[]{:S(2)}, u32[]{:S(2)}) collective-permute-start(bf16[16,64,128]{2,1,0:T(8,128)(2,1)S(1)} %get-tuple-element.158.refs_6_), channel_id=1, source_target_pairs={{0,4},{4,8},{8,12},{12,16},{16,20},{20,24},{24,28},{28,32},{32,36}... | collective-permute-start | bytes 786440 | tf_op jit(solution)/shard_map/ppermute | solution.py:209
  173.9 1.3 copy-start.3
  175.2 27.2 %collective-permute-start = (bf16[32,128,128]{2,1,0:T(8,128)(2,1)S(1)}, bf16[32,128,128]{2,1,0:T(8,128)(2,1)}, u32[]{:S(2)}, u32[]{:S(2)}) collective-permute-start(bf16[32,128,128]{2,1,0:T(8,128)(2,1)S(1)} %get-tuple-element.66.refs_3_), channel_id=1, source_target_pairs={{0,1},{1,2},{2,3},{3,0},{4,5},{5,6},{6,7},{7,4},{8,9},{9,10},{10,1... | collective-permute-start | bytes 3145736 | tf_op jit(solution)/shard_map/cond/branch_1_fun/ppermute | solution.py:293
  178.9 27.4 %collective-permute-start.3 = (bf16[32,128,128]{2,1,0:T(8,128)(2,1)S(1)}, bf16[32,128,128]{2,1,0:T(8,128)(2,1)}, u32[]{:S(2)}, u32[]{:S(2)}) collective-permute-start(bf16[32,128,128]{2,1,0:T(8,128)(2,1)S(1)} %get-tuple-element.67.refs_4_), channel_id=1, source_target_pairs={{0,3},{1,0},{2,1},{3,2},{4,7},{5,4},{6,5},{7,6},{8,11},{9,8},{10,9... | collective-permute-start | bytes 3145736 | tf_op jit(solution)/shard_map/cond/branch_1_fun/ppermute | solution.py:294
  178.9 49.8 %collective-permute-start.2 = (bf16[32,128,128]{2,1,0:T(8,128)(2,1)S(1)}, bf16[32,128,128]{2,1,0:T(8,128)(2,1)}, u32[]{:S(2)}, u32[]{:S(2)}) collective-permute-start(bf16[32,128,128]{2,1,0:T(8,128)(2,1)S(1)} %get-tuple-element.66.refs_3_), channel_id=1, source_target_pairs={{0,3},{1,0},{2,1},{3,2},{4,7},{5,4},{6,5},{7,6},{8,11},{9,8},{10,9... | collective-permute-start | bytes 3145736 | tf_op jit(solution)/shard_map/cond/branch_1_fun/ppermute | solution.py:296
  179.4 49.3 %collective-permute-start.1 = (bf16[32,128,128]{2,1,0:T(8,128)(2,1)S(1)}, bf16[32,128,128]{2,1,0:T(8,128)(2,1)}, u32[]{:S(2)}, u32[]{:S(2)}) collective-permute-start(bf16[32,128,128]{2,1,0:T(8,128)(2,1)S(1)} %get-tuple-element.67.refs_4_), channel_id=1, source_target_pairs={{0,1},{1,2},{2,3},{3,0},{4,5},{5,6},{6,7},{7,4},{8,9},{9,10},{10,1... | collective-permute-start | bytes 3145736 | tf_op jit(solution)/shard_map/cond/branch_1_fun/ppermute | solution.py:295
  202.5 44.3 %collective-permute-start.4 = (bf16[32,128,128]{2,1,0:T(8,128)(2,1)}, bf16[32,128,128]{2,1,0:T(8,128)(2,1)}, u32[]{:S(2)}, u32[]{:S(2)}) collective-permute-start(bf16[32,128,128]{2,1,0:T(8,128)(2,1)} %collective-permute-done.refs_5_), channel_id=1, source_target_pairs={{0,1},{1,2},{2,3},{3,0},{4,5},{5,6},{6,7},{7,4},{8,9},{9,10},{10,1... | collective-permute-start | bytes 3145736 | tf_op jit(solution)/shard_map/cond/branch_1_fun/ppermute | solution.py:201
  206.3 43.9 %collective-permute-start.5 = (bf16[32,128,128]{2,1,0:T(8,128)(2,1)}, bf16[32,128,128]{2,1,0:T(8,128)(2,1)}, u32[]{:S(2)}, u32[]{:S(2)}) collective-permute-start(bf16[32,128,128]{2,1,0:T(8,128)(2,1)} %collective-permute-done.3.refs_8_), channel_id=1, source_target_pairs={{0,3},{1,0},{2,1},{3,2},{4,7},{5,4},{6,5},{7,6},{8,11},{9,8},{10,9... | collective-permute-start | bytes 3145736 | tf_op jit(solution)/shard_map/cond/branch_1_fun/ppermute | solution.py:202
  251.0 10.3 %copy-start.2 = (bf16[32,128,128]{2,1,0:T(8,128)(2,1)S(1)}, bf16[32,128,128]{2,1,0:T(8,128)(2,1)}, u32[]{:S(2)}) copy-start(bf16[32,128,128]{2,1,0:T(8,128)(2,1)} %copy-done.1) | copy-start | bytes 3145732
  251.0 10.3 %copy-start.4 = (bf16[32,128,128]{2,1,0:T(8,128)(2,1)S(1)}, bf16[32,128,128]{2,1,0:T(8,128)(2,1)}, u32[]{:S(2)}) copy-start(bf16[32,128,128]{2,1,0:T(8,128)(2,1)} %copy-done.3) | copy-start | bytes 3145732
  255.3 4.0 %collective-permute-start.16 = (bf16[16,64,128]{2,1,0:T(8,128)(2,1)S(1)}, bf16[16,64,128]{2,1,0:T(8,128)(2,1)S(1)}, u32[]{:S(2)}, u32[]{:S(2)}) collective-permute-start(bf16[16,64,128]{2,1,0:T(8,128)(2,1)S(1)} %get-tuple-element.141.refs_17_), channel_id=1, source_target_pairs={{0,252},{4,0},{8,4},{12,8},{16,12},{20,16},{24,20},{28,24},{32,28}... | collective-permute-start | bytes 786440 | tf_op jit(solution)/shard_map/ppermute | solution.py:211
  255.4 5.9 %collective-permute-start.15 = (bf16[16,64,128]{2,1,0:T(8,128)(2,1)S(1)}, bf16[16,64,128]{2,1,0:T(8,128)(2,1)S(1)}, u32[]{:S(2)}, u32[]{:S(2)}) collective-permute-start(bf16[16,64,128]{2,1,0:T(8,128)(2,1)S(1)} %get-tuple-element.141.refs_17_), channel_id=1, source_target_pairs={{0,4},{4,8},{8,12},{12,16},{16,20},{20,24},{24,28},{28,32},{32,36}... | collective-permute-start | bytes 786440 | tf_op jit(solution)/shard_map/ppermute | solution.py:209
  269.0 4.0 %collective-permute-start.18 = (bf16[16,64,128]{2,1,0:T(8,128)(2,1)S(1)}, bf16[16,64,128]{2,1,0:T(8,128)(2,1)S(1)}, u32[]{:S(2)}, u32[]{:S(2)}) collective-permute-start(bf16[16,64,128]{2,1,0:T(8,128)(2,1)S(1)} %get-tuple-element.145.refs_17_), channel_id=1, source_target_pairs={{0,252},{4,0},{8,4},{12,8},{16,12},{20,16},{24,20},{28,24},{32,28}... | collective-permute-start | bytes 786440 | tf_op jit(solution)/shard_map/ppermute | solution.py:211
  269.1 5.9 %collective-permute-start.17 = (bf16[16,64,128]{2,1,0:T(8,128)(2,1)S(1)}, bf16[16,64,128]{2,1,0:T(8,128)(2,1)S(1)}, u32[]{:S(2)}, u32[]{:S(2)}) collective-permute-start(bf16[16,64,128]{2,1,0:T(8,128)(2,1)S(1)} %get-tuple-element.145.refs_17_), channel_id=1, source_target_pairs={{0,4},{4,8},{8,12},{12,16},{16,20},{20,24},{24,28},{28,32},{32,36}... | collective-permute-start | bytes 786440 | tf_op jit(solution)/shard_map/ppermute | solution.py:209
  283.5 4.0 %collective-permute-start.20 = (bf16[16,64,128]{2,1,0:T(8,128)(2,1)S(1)}, bf16[16,64,128]{2,1,0:T(8,128)(2,1)S(1)}, u32[]{:S(2)}, u32[]{:S(2)}) collective-permute-start(bf16[16,64,128]{2,1,0:T(8,128)(2,1)S(1)} %get-tuple-element.151.refs_17_), channel_id=1, source_target_pairs={{0,252},{4,0},{8,4},{12,8},{16,12},{20,16},{24,20},{28,24},{32,28}... | collective-permute-start | bytes 786440 | tf_op jit(solution)/shard_map/ppermute | solution.py:211
  283.6 5.9 %collective-permute-start.19 = (bf16[16,64,128]{2,1,0:T(8,128)(2,1)S(1)}, bf16[16,64,128]{2,1,0:T(8,128)(2,1)S(1)}, u32[]{:S(2)}, u32[]{:S(2)}) collective-permute-start(bf16[16,64,128]{2,1,0:T(8,128)(2,1)S(1)} %get-tuple-element.151.refs_17_), channel_id=1, source_target_pairs={{0,4},{4,8},{8,12},{12,16},{16,20},{20,24},{24,28},{28,32},{32,36}... | collective-permute-start | bytes 786440 | tf_op jit(solution)/shard_map/ppermute | solution.py:209
  (2 other events, 1.8 us)
